TPU v7x, 32 devices: a whole 2x2x4 slice. The times are simulated.
32 devices in a mesh: rep: 2 (over x), ga: 16 (over z, y, core).
Axes of the slice: x: 2, y: 2, z: 4, core: 2. Of those that a mesh axis runs over, the one named last changes fastest.
Arguments:
- positions: float32 [64, 3, 768], P('rep', None, 'ga'), parts along dimension 0, may hold values from -3 to 23, as said below
- weights: int32 [1, 32], replicated, may hold values from 1 to 16
- psi: bfloat16 [2, 512, 2, 32768], P('rep', None, None, 'ga'), parts along dimension 0, may hold values from -5 to 5
- vloc: float32 [2, 32768], P('rep'), parts along dimension 0, may hold values from -8 to 8
Outputs:
- psi_new: bfloat16 [2, 512, 2, 32768], P('rep', None, None, 'ga'), parts along dimension 0
- bead_forces: float32 [64, 3, 768], P('rep', None, 'ga'), parts along dimension 0
There are 2 independent parts, one for each index of `rep`. A program takes and returns all parts, laid end to end along the dimension named above; an argument that names none is the same for every part. Nothing has to cross between parts.
Inputs may be any that keep to these rules, and one draw needn't show every extreme that they name: `positions`: atom 3w is the oxygen of water w and atoms 3w+1 and 3w+2 are its hydrogens; in every bead each hydrogen lies between 1.0 and 2.6 from its oxygen.
All inputs are finite; a program needn't handle non-finite values.
Results may differ from a plain program's by a relative error of at most 0.0037.
The roundings to bfloat16 on the way count: a program that leaves them out, or rounds other values in their place, can miss the bound.
Values may be sent and summed in bfloat16 or wider, within the bound.
A program may use at most 192 MiB of HBM per device.

v0:
```python
import jax
import jax.numpy as jnp
import numpy as np
from jax import lax
from jax.sharding import PartitionSpec as P

BEADS = 32
CBEADS = 1
WATERS = 256
NGRID = 32
GVECS = 32768
CHUNKS = 2


box_length = 20.0
bond_stiff = 0.5
bond_rest = 1.8
spring_stiff = 2.0
width_square = 0.09
step_size = 0.02
nonlocal_strength = 250.0
occupation = 2.0
highest = lax.Precision.HIGHEST


def frequency(index, count):
    signed = jnp.where(index < count // 2, index, index - count)
    return signed.astype(jnp.float32) * (2.0 * jnp.pi / box_length)


def field_forces(positions):
    oxygen = positions[:, :, 0::3]
    toward_one = positions[:, :, 1::3] - oxygen
    toward_two = positions[:, :, 2::3] - oxygen

    def stretch(offset):
        length = jnp.sqrt(jnp.sum(offset * offset, axis=1, keepdims=True))
        return -bond_stiff * (length - bond_rest) * offset / length

    pull_one = stretch(toward_one)
    pull_two = stretch(toward_two)
    bonds = jnp.stack([-(pull_one + pull_two), pull_one, pull_two], axis=3).reshape(positions.shape)
    springs = 2.0 * positions - jnp.roll(positions, 1, axis=0) - jnp.roll(positions, -1, axis=0)
    return bonds - spring_stiff * springs


def inner(left_mat, right_mat):
    return lax.dot_general(
        left_mat, right_mat, (((1,), (1,)), ((), ())), preferred_element_type=jnp.float32
    )


def real_form(freq_index, group_index):
    product = freq_index[:, None] * freq_index[None, :] % NGRID
    angle = product.astype(jnp.float32) * (2.0 * jnp.pi / NGRID)
    same = (group_index[:, None] == group_index[None, :]).astype(jnp.float32)
    cosines = jnp.cos(angle) * same
    sines = jnp.sin(angle) * same
    return jnp.stack([jnp.stack([cosines, sines], 1), jnp.stack([-sines, cosines], 1)], 0)


def plane_table():
    index = jnp.arange(NGRID, dtype=jnp.int32)
    return real_form(index, jnp.zeros_like(index))


def block_table(length, within):
    index = jnp.arange(length, dtype=jnp.int32)
    if within:
        return real_form(index % NGRID, index // NGRID)
    return real_form(index // NGRID, index % NGRID)


def grid_sum(psi, vloc, parts):
    bands = psi.shape[1]
    local_g = psi.shape[3]
    x_table = plane_table()
    z_table = block_table(local_g, True)
    y_table = block_table(NGRID * NGRID, False)
    grid_potential = vloc[0].reshape(1, 1, NGRID, NGRID * NGRID)
    grouped_raw = psi[0].reshape(parts, bands // parts, 2, local_g)
    planes = lax.all_to_all(grouped_raw, "ga", split_axis=0, concat_axis=3, tiled=True)
    band_count = planes.shape[1]
    blocks_whole = planes.astype(jnp.float32).reshape(band_count, 2, NGRID**3 // local_g, local_g)
    along_z = jnp.einsum("mckp,cpdq->mdkq", blocks_whole, z_table, precision=highest) * (
        1.0 / NGRID
    )
    grid = along_z.reshape(band_count, 2, NGRID, NGRID * NGRID)
    grid = jnp.einsum("mcxr,cxdw->mdwr", grid, x_table, precision=highest) * (1.0 / NGRID)
    grid = jnp.einsum("mcxp,cpdq->mdxq", grid, y_table, precision=highest) * (1.0 / NGRID)
    grid = grid * grid_potential
    grid = jnp.einsum("mdxq,cpdq->mcxp", grid, y_table, precision=highest)
    grid = jnp.einsum("mdwr,cxdw->mcxr", grid, x_table, precision=highest)
    returning = grid.reshape(1, band_count, 2, NGRID**3)
    returned = lax.all_to_all(
        returning.astype(jnp.bfloat16), "ga", split_axis=3, concat_axis=0, tiled=True
    ).astype(returning.dtype)
    returned = returned.reshape(bands, 2, local_g)
    potential = jnp.einsum("bdq,cpdq->bcp", returned, z_table, precision=highest)
    return potential[:, 0], potential[:, 1]


def plane_rotation():
    small = np.arange(NGRID)
    angle = small[:, None] * small[None, :] % NGRID * (2.0 * np.pi / NGRID)
    side = NGRID * NGRID
    wave = np.kron(np.exp(1j * angle), np.exp(1j * angle))
    real, imag = np.real(wave), np.imag(wave)
    table = np.stack([np.stack([real, -imag], 1), np.stack([imag, real], 1)], 1)
    return jnp.asarray(table.reshape(2 * side, 2 * side).astype(np.float32), jnp.bfloat16)


def line_rotation(group):
    small = np.arange(NGRID)
    angle = small[:, None] * small[None, :] % NGRID * (2.0 * np.pi / NGRID)
    real, imag = np.cos(angle), np.sin(angle)
    form = np.stack([np.stack([real, -imag], 2), np.stack([imag, real], 2)], 1)
    same = np.eye(group)
    table = form[:, None, :, :, None, :] * same[None, :, None, None, :, None]
    size = 2 * NGRID * group
    return jnp.asarray(table.reshape(size, size).astype(np.float32), jnp.bfloat16)


def plane_out(psi, parts, plane_table, offset):
    bands = psi.shape[1]
    side = NGRID * NGRID
    planes = psi.shape[3] // side
    chunk = bands // CHUNKS
    pieces = []
    for first in range(0, bands, chunk):
        part = lax.dynamic_slice_in_dim(psi[0], first + offset, chunk, axis=0).reshape(chunk, 2, planes, side)
        part = part.transpose(2, 0, 1, 3).reshape(planes, chunk, 2 * side)
        pieces.append(
            jnp.stack(
                [
                    jnp.einsum(
                        "qk,bk->qb", plane_table, part[p], preferred_element_type=jnp.float32
                    )
                    .astype(jnp.bfloat16)
                    .reshape(parts, 2 * side // parts, chunk)
                    for p in range(planes)
                ],
                1,
            )
        )
    return pieces


def exchange(piece):
    return lax.all_to_all(piece, "ga", split_axis=0, concat_axis=0, tiled=True)


def line_action(vloc, parts):
    side = NGRID * NGRID
    points = side // parts
    group = min(8, points)
    groups = points // group
    line_table = line_rotation(group)
    start = lax.axis_index("ga") * points
    own = lax.dynamic_slice_in_dim(vloc[0].reshape(NGRID, side), start, points, axis=1)
    own = own.reshape(NGRID, groups, group).transpose(1, 0, 2) * (1.0 / (NGRID * side))
    own = jnp.broadcast_to(own[..., None], (groups, NGRID, group, 2)).reshape(groups, -1, 1)
    scaled = (own * line_table.astype(jnp.float32)).astype(jnp.bfloat16)
    return jnp.einsum(
        "ea,gec->gac", line_table, scaled, preferred_element_type=jnp.float32
    ).astype(jnp.bfloat16)


def line_step(action, lines):
    parts, planes, rows, chunk = lines.shape
    groups = action.shape[0]
    lines = lines.reshape(parts * planes, groups, rows // groups, chunk)
    lines = lines.transpose(1, 0, 2, 3).reshape(groups, -1, chunk)
    lines = jnp.einsum(
        "gac,gcb->gab", action, lines, preferred_element_type=jnp.float32
    ).astype(jnp.bfloat16)
    lines = lines.reshape(groups, parts * planes, rows // groups, chunk).transpose(1, 0, 2, 3)
    return lines.reshape(parts, planes, rows, chunk)


def plane_back(backs, plane_table):
    side = NGRID * NGRID
    reals, imags = [], []
    for back in backs:
        chunk = back.shape[3]
        whole = [
            jnp.einsum(
                "qb,qk->bk",
                back[:, p].reshape(2 * side, chunk),
                plane_table,
                preferred_element_type=jnp.float32,
            )
            for p in range(back.shape[1])
        ]
        reals.append(jnp.concatenate([w[:, :side] for w in whole], 1))
        imags.append(jnp.concatenate([w[:, side:] for w in whole], 1))
    return jnp.concatenate(reals, 0), jnp.concatenate(imags, 0)


def waves(oxygens, gvectors, profile):
    local_g = profile.shape[0]
    side = NGRID * NGRID
    if local_g % side:
        phases = jnp.einsum("ai,ag->ig", oxygens, gvectors, precision=highest)
        return profile * jnp.cos(phases), profile * jnp.sin(phases)
    spots = oxygens.T
    flat = spots[:, 1:2] * gvectors[1:2, :side] + spots[:, 2:3] * gvectors[2:3, :side]
    flat_cos, flat_sin = jnp.cos(flat), jnp.sin(flat)
    along = spots[:, 0:1] * gvectors[0:1, ::side]
    along_cos, along_sin = jnp.cos(along), jnp.sin(along)
    cosines, sines = [], []
    for p in range(local_g // side):
        c, s = along_cos[:, p : p + 1], along_sin[:, p : p + 1]
        cosines.append(c * flat_cos - s * flat_sin)
        sines.append(s * flat_cos + c * flat_sin)
    return profile * jnp.concatenate(cosines, 1), profile * jnp.concatenate(sines, 1)


def per_device(positions, weights, psi, vloc):
    near_forces = field_forces(positions)
    weight_float = weights.astype(jnp.float32)
    mixing = weight_float / jnp.sum(weight_float, axis=1, keepdims=True)
    centres = jnp.einsum("cj,jan->can", mixing, positions, precision=highest)
    parts = lax.axis_size("ga")
    near_oxygen = centres[0][:, 0::3]
    own_waters = near_oxygen.shape[1]
    everyone = lax.dynamic_update_slice(
        jnp.zeros((3, own_waters * parts), jnp.float32),
        near_oxygen,
        (0, lax.axis_index("ga") * own_waters),
    )
    oxygens = lax.psum(everyone, "ga")
    side = NGRID * NGRID
    whole_planes = psi.shape[3] % side == 0 and side % parts == 0
    if whole_planes:
        plane_table = plane_rotation()
        pieces = plane_out(psi, parts, plane_table, (oxygens[0, 0] * 0.0).astype(jnp.int32))
        lines = [exchange(piece) for piece in pieces]
        action = line_action(vloc, parts)
    bands = psi.shape[1]
    local_g = psi.shape[3]
    flat_index = lax.axis_index("ga") * local_g + jnp.arange(local_g, dtype=jnp.int32)
    gvectors = jnp.stack(
        [
            frequency(flat_index // (NGRID * NGRID), NGRID),
            frequency(flat_index // NGRID % NGRID, NGRID),
            frequency(flat_index % NGRID, NGRID),
        ]
    )
    square = jnp.sum(gvectors * gvectors, axis=0)
    profile = jnp.exp(-0.5 * width_square * square)
    kinetic = 0.5 * square
    wave_cos, wave_sin = waves(oxygens, gvectors, profile)
    table = jnp.concatenate(
        [jnp.concatenate([wave_cos, -wave_sin], 1), jnp.concatenate([wave_sin, wave_cos], 1)], 0
    ).astype(jnp.bfloat16)
    wavefunc = psi[0].reshape(bands, 2 * local_g)
    partial_proj = (inner(table, wavefunc) * (1.0 / GVECS)).reshape(2, WATERS, bands)
    share = lax.psum_scatter(partial_proj, "ga", scatter_dimension=1, tiled=True).astype(
        jnp.bfloat16
    )
    table_blocks = table.reshape(2 * WATERS, 2 * local_g)
    copies = jnp.broadcast_to(share[None], (parts,) + share.shape)
    if whole_planes:
        lines[-1], copies = lax.optimization_barrier((lines[-1], copies))
    all_proj = lax.all_to_all(copies, "ga", split_axis=0, concat_axis=0, tiled=True)
    if whole_planes:
        moved = [line_step(action, line) for line in lines]
        moved[0], all_proj = lax.optimization_barrier((moved[0], all_proj))
        backs = [exchange(piece) for piece in moved]
    all_proj = all_proj.transpose(1, 0, 2, 3).reshape(2 * WATERS, bands)
    nonlocal_term = jnp.einsum(
        "ib,ig->bg", all_proj, table_blocks, preferred_element_type=jnp.float32
    )
    crossed = jnp.dot(all_proj, wavefunc, preferred_element_type=jnp.float32)
    weighted_re = crossed[:WATERS, :local_g] + crossed[WATERS:, local_g:]
    weighted_im = crossed[:WATERS, local_g:] - crossed[WATERS:, :local_g]
    mixed_wave = wave_cos * weighted_im + wave_sin * weighted_re
    force_part = (
        2.0
        * occupation
        * nonlocal_strength
        / GVECS
        * jnp.einsum("ag,ig->ai", gvectors, mixed_wave, precision=highest)
    )
    force_rows = force_part.reshape(3, parts, own_waters).transpose(1, 0, 2)
    force_rows = force_rows.reshape(parts, 1, 3 * own_waters)
    force_rows = jnp.pad(force_rows, ((0, 0), (0, 0), (0, bands - 3 * own_waters)))
    wave_float = psi[0].astype(jnp.float32)
    if whole_planes:
        potential = plane_back(backs, plane_table)
    else:
        potential = grid_sum(psi, vloc, parts)
    hamil_re = (
        kinetic * wave_float[:, 0]
        + potential[0]
        + nonlocal_strength * nonlocal_term[:, :local_g]
    )
    hamil_im = (
        kinetic * wave_float[:, 1]
        + potential[1]
        + nonlocal_strength * nonlocal_term[:, local_g:]
    )
    trial_re = (wave_float[:, 0] - step_size * hamil_re).astype(jnp.bfloat16)
    trial_im = (wave_float[:, 1] - step_size * hamil_im).astype(jnp.bfloat16)
    row = lax.broadcasted_iota(jnp.int32, (bands, bands), 0)
    column = lax.broadcasted_iota(jnp.int32, (bands, bands), 1)
    even = inner(trial_re, trial_re) + inner(trial_im, trial_im)
    odd = inner(trial_im, trial_re) - inner(trial_re, trial_im)
    packed = jnp.where(row <= column, even, odd) * (1.0 / GVECS)
    shares = lax.all_to_all(
        jnp.concatenate([packed.reshape(parts, bands // parts, bands), force_rows], 1),
        "ga",
        split_axis=0,
        concat_axis=0,
        tiled=True,
    )
    sums = jnp.sum(shares, axis=0)
    oxygen_force = sums[-1, : 3 * own_waters].reshape(3, own_waters)
    hydrogen_zero = jnp.zeros_like(oxygen_force)
    dft_forces = [jnp.stack([oxygen_force, hydrogen_zero, hydrogen_zero], axis=2).reshape(3, -1)]
    own_rows = lax.broadcasted_iota(jnp.int32, (bands // parts, bands), 0) + lax.axis_index(
        "ga"
    ) * (bands // parts)
    own_columns = lax.broadcasted_iota(jnp.int32, (bands // parts, bands), 1)
    mixed_rows = jnp.where(own_rows == own_columns, 1.5, 0.0) - 0.5 * sums[:-1]
    mixed = lax.all_gather(mixed_rows.astype(jnp.bfloat16), "ga", axis=0, tiled=True)
    turned = mixed.T
    mix_re = jnp.where(row <= column, mixed, turned)
    mix_im = jnp.where(row > column, mixed, jnp.where(row < column, -turned, jnp.zeros_like(turned)))
    both = jnp.concatenate([trial_re, trial_im], 0)
    new_re = jnp.dot(
        jnp.concatenate([mix_re, -mix_im], 1), both, preferred_element_type=jnp.float32
    ).astype(jnp.bfloat16)
    new_im = jnp.dot(
        jnp.concatenate([mix_im, mix_re], 1), both, preferred_element_type=jnp.float32
    ).astype(jnp.bfloat16)
    new_waves = [jnp.stack([new_re, new_im], 1)]
    contracted_force = jnp.einsum("cj,can->jan", mixing, jnp.stack(dft_forces), precision=highest)
    bead_forces = near_forces + BEADS / CBEADS * contracted_force
    return (jnp.stack(new_waves), bead_forces)


def solution(mesh):
    placed = (P("rep", None, "ga"), P(), P("rep", None, None, "ga"), P("rep", None))
    return jax.shard_map(
        per_device,
        mesh=mesh,
        in_specs=placed,
        out_specs=(P("rep", None, None, "ga"), P("rep", None, "ga")),
        check_vma=False,
    )
```

profile of v0, /device:TPU:0, one launch (start us, length us, event | category | flops | bytes accessed | tf_op | source)
XLA Modules:
  0.0 449.7 jit_solution(4897003384175119418)
XLA Ops:
  10.3 35.0 %psum.7 = f32[3,256]{1,0:T(4,128)S(1)} all-reduce(f32[3,256]{1,0:T(4,128)S(1)} %dynamic_update_slice.3), channel_id=1, replica_groups=mesh['rep'=2,'ga'=16] {'ga'}, use_global_device_ids=true, to_apply=%region_2.3 | all-reduce | flops 768 | bytes 6144 | tf_op jit(solution)/shard_map/psum | solution.py:232
  46.6 6.4 %constant_dynamic-slice_fusion = (bf16[1,256,2,2048]{3,2,1,0:T(2,128)(2,1)}, bf16[1,256,2,2048]{3,2,1,0:T(2,128)(2,1)S(1)}) fusion(bf16[1,512,2,2048]{3,2,1,0:T(2,128)(2,1)} %param.8, s32[]{:T(128)S(6)} %select_n.118, s32[]{:T(128)S(6)} %select_n.117), kind=kLoop, calls=%fused_computation.132 | loop fusion | bytes 8388616 | tf_op jit(solution)/shard_map/dynamic_slice | solution.py:131
  53.0 6.1 %copy.108 = bf16[1,256,2,2048]{1,3,2,0:T(8,128)(2,1)} copy(bf16[1,256,2,2048]{3,2,1,0:T(2,128)(2,1)} %get-tuple-element.26) | data formatting | bytes 4194304
  59.1 2.6 fusion.79
  61.8 6.8 %fusion.16 = bf16[2048,256]{0,1:T(8,128)(2,1)} fusion(bf16[256,2048]{0,1:T(8,128)(2,1)S(1)} %bitcast.175, bf16[2048,2048]{1,0:T(8,128)(2,1)} %constant.111.clone), kind=kOutput, calls=%fused_computation.33 | convolution fusion | flops 2148007936 | bytes 10485760 | tf_op jit(solution)/shard_map/qk,bk->qb/dot_general | solution.py:136
  70.0 7.1 %fusion.17 = bf16[2048,256]{0,1:T(8,128)(2,1)} fusion(bf16[256,2048]{0,1:T(8,128)(2,1)} %bitcast.173, bf16[2048,2048]{1,0:T(8,128)(2,1)} %constant.111.clone), kind=kOutput, calls=%fused_computation.34 | convolution fusion | flops 2148007936 | bytes 10485760 | tf_op jit(solution)/shard_map/qk,bk->qb/dot_general | solution.py:136
  77.1 2.3 copy.106
  79.4 2.8 pad_maximum_fusion.4
  82.2 4.7 %all-to-all-start.1 = ((bf16[16,2,128,256]{3,2,1,0:T(8,128)(2,1)}), bf16[16,2,128,256]{3,2,1,0:T(8,128)(2,1)}, u32[]{:S(2)}, u32[]{:S(2)}) async-start(bf16[16,2,128,256]{3,2,1,0:T(8,128)(2,1)} %pad_maximum_fusion.4), calls=%async_computation.1 | async-start | bytes 4194304 | tf_op jit(solution)/shard_map/all_to_all | solution.py:150
  87.1 4.1 copy.107
  91.2 2.6 fusion.80
  93.9 5.8 %fusion.14 = bf16[2048,256]{0,1:T(8,128)(2,1)S(1)} fusion(bf16[256,2048]{0,1:T(8,128)(2,1)S(1)} %bitcast.176, bf16[2048,2048]{1,0:T(8,128)(2,1)} %constant.111.clone), kind=kOutput, calls=%fused_computation.31 | convolution fusion | flops 2148007936 | bytes 10485760 | tf_op jit(solution)/shard_map/qk,bk->qb/dot_general | solution.py:136
  100.2 6.1 %fusion.15 = bf16[2048,256]{0,1:T(8,128)(2,1)S(1)} fusion(bf16[256,2048]{0,1:T(8,128)(2,1)} %bitcast.174, bf16[2048,2048]{1,0:T(8,128)(2,1)} %constant.111.clone), kind=kOutput, calls=%fused_computation.32 | convolution fusion | flops 2148007936 | bytes 10485760 | tf_op jit(solution)/shard_map/qk,bk->qb/dot_general | solution.py:136
  106.8 6.6 %copy.111 = bf16[64,8,2,2048]{3,1,2,0:T(8,128)(2,1)} copy(bf16[64,8,2,2048]{3,2,1,0:T(2,128)(2,1)} %bitcast.149) | data formatting | bytes 8388608
  115.1 12.7 %all-to-all-done.1 = bf16[16,2,128,256]{3,2,1,0:T(8,128)(2,1)} async-done(((bf16[16,2,128,256]{3,2,1,0:T(8,128)(2,1)}), bf16[16,2,128,256]{3,2,1,0:T(8,128)(2,1)}, u32[]{:S(2)}, u32[]{:S(2)}) %all-to-all-start.1) | async-done | bytes 2097184 | tf_op jit(solution)/shard_map/all_to_all | solution.py:150
  127.8 11.2 %all-to-all-start = ((bf16[16,2,128,256]{3,2,1,0:T(8,128)(2,1)}), bf16[16,2,128,256]{3,2,1,0:T(8,128)(2,1)S(1)}, u32[]{:S(2)}, u32[]{:S(2)}) async-start(bf16[16,2,128,256]{3,2,1,0:T(8,128)(2,1)} %pad_maximum_fusion.3), calls=%async_computation | async-start | bytes 4194304 | tf_op jit(solution)/shard_map/all_to_all | solution.py:150
  140.1 4.2 multiply_add_fusion.1
  146.0 2.8 copy-done
  148.8 3.4 convolution_multiply_fusion
  153.7 58.1 %reduce-scatter.2.cloned.1.call-done = f32[2,16,512]{2,1,0:T(8,128)} async-done(((f32[2,256,512]{2,1,0:T(8,128)}), f32[2,16,512]{2,1,0:T(8,128)}) %reduce-scatter.2.cloned.1.call-update) | async-done | bytes 65552 | tf_op jit(solution)/shard_map/reduce_scatter | solution.py:259
  213.5 4.2 all-to-all-start.2
  218.2 3.7 fusion.13
  222.0 3.3 copy.84
  226.8 1.6 copy.86
  228.4 3.7 all-to-all-done.2
  232.0 4.6 %all-to-all-start.4 = ((bf16[16,2,128,256]{3,2,1,0:T(8,128)(2,1)}), bf16[16,2,128,256]{3,2,1,0:T(8,128)(2,1)}, u32[]{:S(2)}, u32[]{:S(2)}) async-start(bf16[16,2,128,256]{3,2,1,0:T(8,128)(2,1)} %bitcast.153), calls=%async_computation.5 | async-start | bytes 4194304 | tf_op jit(solution)/shard_map/all_to_all | solution.py:150
  236.6 7.5 %bitcast_convert_fusion = f32[512,2,2048]{2,0,1:T(8,128)} fusion(bf16[1,512,2,2048]{3,2,1,0:T(2,128)(2,1)} %param.8), kind=kLoop, calls=%fused_computation.19 | loop fusion | flops 2097152 | bytes 12582912 | tf_op jit(solution)/shard_map/convert_element_type | solution.py:289
  244.3 2.0 copy-done.3
  251.7 5.6 %fusion.92 = f32[512,4096]{1,0:T(8,128)} fusion(bf16[512,512]{1,0:T(8,128)(2,1)S(1)} %bitcast.168, bf16[512,4096]{1,0:T(8,128)(2,1)S(1)} %bitcast.151), kind=kOutput, calls=%fused_computation.168 | convolution fusion | flops 2147483648 | bytes 13107200 | tf_op jit(solution)/shard_map/dot_general | solution.py:275
  257.4 20.3 %all-to-all-done.4 = bf16[16,2,128,256]{3,2,1,0:T(8,128)(2,1)} async-done(((bf16[16,2,128,256]{3,2,1,0:T(8,128)(2,1)}), bf16[16,2,128,256]{3,2,1,0:T(8,128)(2,1)}, u32[]{:S(2)}, u32[]{:S(2)}) %all-to-all-start.4) | async-done | bytes 2097184 | tf_op jit(solution)/shard_map/all_to_all | solution.py:150
  277.6 11.2 %all-to-all-start.3 = ((bf16[16,2,128,256]{3,2,1,0:T(8,128)(2,1)}), bf16[16,2,128,256]{3,2,1,0:T(8,128)(2,1)S(1)}, u32[]{:S(2)}, u32[]{:S(2)}) async-start(bf16[16,2,128,256]{3,2,1,0:T(8,128)(2,1)} %bitcast.24), calls=%async_computation.4 | async-start | bytes 4194304 | tf_op jit(solution)/shard_map/all_to_all | solution.py:150
  288.8 6.3 %fusion.30 = f32[3,256]{1,0:T(4,128)S(1)} fusion(f32[512,4096]{1,0:T(8,128)} %fusion.92, f32[256,1024]{1,0:T(8,128)} %copy-done.5, f32[256,1024]{1,0:T(8,128)} %copy-done.4, f32[256,1024]{1,0:T(8,128)} %copy-done.6, f32[256,1024]{1,0:T(8,128)S(1)} %get-tuple-element.60, f32[2048]{0:T(1024)S(1)} %copy-done.24, f32[1,2048]{1,0:T(1,128)S(1)} %copy-done.20, ...), kind=kOutput, calls=%fused_computation.59 | convolution fusion | flops 23606016 | bytes 12618752 | tf_op jit(solution)/shard_map/ag,ig->ai/dot_general | solution.py:284
  295.4 8.0 %fusion.29 = f32[512,4096]{1,0:T(8,128)} fusion(bf16[512,512]{1,0:T(8,128)(2,1)} %bitcast.169, bf16[256,2048]{1,0:T(8,128)(2,1)} %copy-done.17, bf16[256,2048]{1,0:T(8,128)(2,1)} %copy-done.16, bf16[256,2048]{1,0:T(8,128)(2,1)} %copy-done.15), kind=kOutput, calls=%fused_computation.58 | convolution fusion | flops 2164260864 | bytes 12058624 | tf_op jit(solution)/shard_map/ib,ig->bg/dot_general | solution.py:272
  303.3 1.8 fusion.78
  305.2 5.9 %fusion.89 = f32[256,2048]{1,0:T(8,128)S(1)} fusion(bf16[2048,256]{1,0:T(8,128)(2,1)S(1)} %bitcast.162, bf16[2048,2048]{1,0:T(8,128)(2,1)} %constant.111.clone), kind=kOutput, calls=%fused_computation.165 | convolution fusion | flops 2147483648 | bytes 11534336 | tf_op jit(solution)/shard_map/qb,qk->bk/dot_general | solution.py:187
  312.3 2.3 fusion.88
  316.1 13.7 %all-to-all-done.3 = bf16[16,2,128,256]{3,2,1,0:T(8,128)(2,1)S(1)} async-done(((bf16[16,2,128,256]{3,2,1,0:T(8,128)(2,1)}), bf16[16,2,128,256]{3,2,1,0:T(8,128)(2,1)S(1)}, u32[]{:S(2)}, u32[]{:S(2)}) %all-to-all-start.3) | async-done | bytes 2097184 | tf_op jit(solution)/shard_map/all_to_all | solution.py:150
  330.0 5.9 %fusion.87 = f32[256,2048]{1,0:T(8,128)S(1)} fusion(bf16[2048,256]{1,0:T(8,128)(2,1)S(1)} %bitcast.163, bf16[2048,2048]{1,0:T(8,128)(2,1)} %constant.111.clone), kind=kOutput, calls=%fused_computation.163 | convolution fusion | flops 2147483648 | bytes 11534336 | tf_op jit(solution)/shard_map/qb,qk->bk/dot_general | solution.py:187
  336.1 2.3 fusion.86
  340.7 10.8 %fusion.8 = (bf16[512,2048]{1,0:T(8,128)(2,1)}, bf16[512,2048]{1,0:T(8,128)(2,1)}) fusion(f32[512,4096]{1,0:T(8,128)} %fusion.29, f32[256,1024]{1,0:T(8,128)S(1)} %get-tuple-element.36, f32[256,1024]{1,0:T(8,128)S(1)} %copy-done.8, f32[256,1024]{1,0:T(8,128)S(1)} %get-tuple-element.32, f32[256,1024]{1,0:T(8,128)S(1)} %get-tuple-element.30, ...), kind=kLoop, calls=%fused_computation.12 | loop fusion | flops 20971520 | bytes 29368320 | tf_op jit(solution)/shard_map/convert_element_type | solution.py:304
  351.5 3.7 fusion.90
  360.3 11.2 %all-to-all-start.5 = ((f32[16,33,512]{2,1,0:T(8,128)}), f32[16,33,512]{2,1,0:T(8,128)S(1)}, u32[]{:S(2)}, u32[]{:S(2)}) async-start(f32[16,33,512]{2,1,0:T(8,128)} %select_maximum_fusion), calls=%async_computation.6 | async-start | bytes 2621440 | tf_op jit(solution)/shard_map/all_to_all | solution.py:311
  375.9 1.7 copy.91
  381.9 16.9 %all-to-all-done.5 = f32[16,33,512]{2,1,0:T(8,128)S(1)} async-done(((f32[16,33,512]{2,1,0:T(8,128)}), f32[16,33,512]{2,1,0:T(8,128)S(1)}, u32[]{:S(2)}, u32[]{:S(2)}) %all-to-all-start.5) | async-done | bytes 1081376 | tf_op jit(solution)/shard_map/all_to_all | solution.py:311
  403.2 25.5 %all_gather.3 = bf16[512,512]{1,0:T(8,128)(2,1)S(1)} all-gather(bf16[32,512]{1,0:T(8,128)(2,1)S(1)} %fusion.51), channel_id=1, replica_groups=mesh['rep'=2,'ga'=16] {'ga'}, dimensions={0}, use_global_device_ids=true | all-gather | bytes 557056 | tf_op jit(solution)/shard_map/all_gather | solution.py:327
  429.2 4.1 fusion.11
  433.4 2.4 fusion.12
  436.1 6.3 %copy.98 = bf16[1,512,2,2048]{3,2,1,0:T(2,128)(2,1)} copy(bf16[1,512,2,2048]{3,1,2,0:T(8,128)(2,1)S(1)} %maximum_bitcast_fusion) | data formatting | bytes 8388608
  (142 shorter events, 46.2 us)
Async XLA Ops:
  82.2 45.6 %all-to-all-start.1 = ((bf16[16,2,128,256]{3,2,1,0:T(8,128)(2,1)}), bf16[16,2,128,256]{3,2,1,0:T(8,128)(2,1)}, u32[]{:S(2)}, u32[]{:S(2)}) async-start(bf16[16,2,128,256]{3,2,1,0:T(8,128)(2,1)} %pad_maximum_fusion.4), calls=%async_computation.1 | async-start | bytes 4194304 | tf_op jit(solution)/shard_map/all_to_all | solution.py:150
  86.9 26.5 %copy-start.19 = (f32[1,2048]{1,0:T(1,128)}, f32[1,2048]{1,0:T(1,128)S(1)}, u32[]{:S(2)}) copy-start(f32[1,2048]{1,0:T(1,128)S(1)} %fusion.58) | copy-start | bytes 24580
  87.0 26.4 %copy-start.21 = (f32[1,2048]{1,0:T(1,128)}, f32[1,2048]{1,0:T(1,128)S(1)}, u32[]{:S(2)}) copy-start(f32[1,2048]{1,0:T(1,128)S(1)} %get-tuple-element.80) | copy-start | bytes 24580
  113.5 26.6 %slice-start.4 = ((f32[1,2048]{1,0:T(1,128)}), f32[1,1024]{1,0:T(1,128)S(1)}, s32[]{:S(2)}) async-start(f32[1,2048]{1,0:T(1,128)} %copy-done.19), calls=%async_computation.12 | async-start | bytes 8192 | tf_op jit(solution)/shard_map/slice | solution.py:207
  127.8 85.7 %all-to-all-start = ((bf16[16,2,128,256]{3,2,1,0:T(8,128)(2,1)}), bf16[16,2,128,256]{3,2,1,0:T(8,128)(2,1)S(1)}, u32[]{:S(2)}, u32[]{:S(2)}) async-start(bf16[16,2,128,256]{3,2,1,0:T(8,128)(2,1)} %pad_maximum_fusion.3), calls=%async_computation | async-start | bytes 4194304 | tf_op jit(solution)/shard_map/all_to_all | solution.py:150
  139.0 72.8 %reduce-scatter.2.cloned.1.call-start = ((), (), s32[]{:S(2)}) async-start(), calls=%async_computation.7 | async-start | bytes 1114112 | tf_op jit(solution)/shard_map/reduce_scatter | solution.py:259
  140.1 5.9 %copy-start.23 = (f32[2048]{0:T(1024)}, f32[2048]{0:T(1024)S(1)}, u32[]{:S(2)}) copy-start(f32[2048]{0:T(1024)S(1)} %get-tuple-element.67) | copy-start | bytes 24580
  144.3 1.0 copy-start.4
  144.3 1.7 copy-start.5
  144.3 1.7 copy-start.6
  144.3 4.5 copy-start
  146.0 6.2 %copy-start.15 = (bf16[256,2048]{1,0:T(8,128)(2,1)}, bf16[256,2048]{1,0:T(8,128)(2,1)S(1)}, u32[]{:S(2)}) copy-start(bf16[256,2048]{1,0:T(8,128)(2,1)S(1)} %get-tuple-element.28) | copy-start | bytes 3145732
  146.0 6.1 %copy-start.16 = (bf16[256,2048]{1,0:T(8,128)(2,1)}, bf16[256,2048]{1,0:T(8,128)(2,1)S(1)}, u32[]{:S(2)}) copy-start(bf16[256,2048]{1,0:T(8,128)(2,1)S(1)} %get-tuple-element.29) | copy-start | bytes 3145732
  146.0 6.1 %copy-start.17 = (bf16[256,2048]{1,0:T(8,128)(2,1)}, bf16[256,2048]{1,0:T(8,128)(2,1)S(1)}, u32[]{:S(2)}) copy-start(bf16[256,2048]{1,0:T(8,128)(2,1)S(1)} %get-tuple-element.68) | copy-start | bytes 3145732
  148.8 4.0 copy-start.18
  213.5 18.5 %all-to-all-start.2 = ((bf16[16,2,16,512]{3,2,1,0:T(8,128)(2,1)}), bf16[16,2,16,512]{3,2,1,0:T(8,128)(2,1)}, u32[]{:S(2)}, u32[]{:S(2)}) async-start(bf16[16,2,16,512]{3,2,1,0:T(8,128)(2,1)} %broadcast_in_dim.18), calls=%async_computation.3 | async-start | bytes 1048576 | tf_op jit(solution)/shard_map/all_to_all | solution.py:266
  222.0 4.8 %copy-start.2 = (bf16[8,512,512]{2,1,0:T(8,128)(2,1)}, bf16[8,512,512]{2,1,0:T(8,128)(2,1)S(1)}, u32[]{:S(2)}) copy-start(bf16[8,512,512]{2,1,0:T(8,128)(2,1)S(1)} %fusion.13) | copy-start | bytes 12582916
  232.0 45.6 %all-to-all-start.4 = ((bf16[16,2,128,256]{3,2,1,0:T(8,128)(2,1)}), bf16[16,2,128,256]{3,2,1,0:T(8,128)(2,1)}, u32[]{:S(2)}, u32[]{:S(2)}) async-start(bf16[16,2,128,256]{3,2,1,0:T(8,128)(2,1)} %bitcast.153), calls=%async_computation.5 | async-start | bytes 4194304 | tf_op jit(solution)/shard_map/all_to_all | solution.py:150
  244.1 2.2 copy-start.3
  247.9 3.9 copy-start.1
  251.0 0.8 copy-start.10
  257.3 31.5 %copy-start.20 = (f32[1,2048]{1,0:T(1,128)S(1)}, f32[1,2048]{1,0:T(1,128)}, u32[]{:S(2)}) copy-start(f32[1,2048]{1,0:T(1,128)} %copy-done.19) | copy-start | bytes 24580
  257.4 31.5 %copy-start.22 = (f32[1,2048]{1,0:T(1,128)S(1)}, f32[1,2048]{1,0:T(1,128)}, u32[]{:S(2)}) copy-start(f32[1,2048]{1,0:T(1,128)} %copy-done.21) | copy-start | bytes 24580
  257.4 31.5 %copy-start.24 = (f32[2048]{0:T(1024)S(1)}, f32[2048]{0:T(1024)}, u32[]{:S(2)}) copy-start(f32[2048]{0:T(1024)} %copy-done.23) | copy-start | bytes 24580
  277.6 52.2 %all-to-all-start.3 = ((bf16[16,2,128,256]{3,2,1,0:T(8,128)(2,1)}), bf16[16,2,128,256]{3,2,1,0:T(8,128)(2,1)S(1)}, u32[]{:S(2)}, u32[]{:S(2)}) async-start(bf16[16,2,128,256]{3,2,1,0:T(8,128)(2,1)} %bitcast.24), calls=%async_computation.4 | async-start | bytes 4194304 | tf_op jit(solution)/shard_map/all_to_all | solution.py:150
  303.3 8.9 %slice-start = ((s8[8388608]{0:T(1024)(128)(4,1)}), s8[4194304]{0:T(1024)(128)(4,1)S(1)}, s32[]{:S(2)}) async-start(s8[8388608]{0:T(1024)(128)(4,1)} %bitcast.145), calls=%async_computation.8 | async-start | bytes 8388608
  305.2 7.1 %slice-start.1 = ((s8[8388608]{0:T(1024)(128)(4,1)}), s8[4194304]{0:T(1024)(128)(4,1)S(1)}, s32[]{:S(2)}) async-start(s8[8388608]{0:T(1024)(128)(4,1)} %bitcast.145), calls=%async_computation.9 | async-start | bytes 8388608
  329.8 6.3 %slice-start.2 = ((s8[8388608]{0:T(1024)(128)(4,1)}), s8[4194304]{0:T(1024)(128)(4,1)S(1)}, s32[]{:S(2)}) async-start(s8[8388608]{0:T(1024)(128)(4,1)} %bitcast.147), calls=%async_computation.10 | async-start | bytes 8388608
  330.0 6.1 %slice-start.3 = ((s8[8388608]{0:T(1024)(128)(4,1)}), s8[4194304]{0:T(1024)(128)(4,1)S(1)}, s32[]{:S(2)}) async-start(s8[8388608]{0:T(1024)(128)(4,1)} %bitcast.147), calls=%async_computation.11 | async-start | bytes 8388608
  338.4 1.5 copy-start.7
  338.4 1.9 copy-start.8
  338.5 2.2 copy-start.9
  338.5 2.2 copy-start.25
  351.5 3.7 copy-start.11
  351.5 3.7 copy-start.12
  359.1 12.5 %copy-start.14 = (f32[32,3,48]{2,0,1:T(8,128)S(1)}, f32[32,3,48]{2,0,1:T(8,128)}, u32[]{:S(2)}) copy-start(f32[32,3,48]{2,0,1:T(8,128)} %param.6) | copy-start | bytes 55300
  359.1 21.5 %copy-start.26 = (s32[1,32]{1,0:T(1,128)S(1)}, s32[1,32]{1,0:T(1,128)}, u32[]{:S(2)}) copy-start(s32[1,32]{1,0:T(1,128)} %param.7) | copy-start | bytes 388
  360.3 38.5 %all-to-all-start.5 = ((f32[16,33,512]{2,1,0:T(8,128)}), f32[16,33,512]{2,1,0:T(8,128)S(1)}, u32[]{:S(2)}, u32[]{:S(2)}) async-start(f32[16,33,512]{2,1,0:T(8,128)} %select_maximum_fusion), calls=%async_computation.6 | async-start | bytes 2621440 | tf_op jit(solution)/shard_map/all_to_all | solution.py:311
  429.2 4.2 copy-start.13
Sparse Core Ops, SparseCore 0:
  152.3 59.4 reduce-scatter.1
where the time goes:
time: 458 us; the launch traced here: 450 us
  waiting for transfers between devices  125 us (27%)
  matrix products  87.9 us (19%)
  local copies, waits for them, and re-layouts  74.3 us (16%)
  blocking collectives  60.5 us (13%)
  starting transfers between devices  47.6 us (10%)
  other arithmetic  38.4 us (8%)
  between operations  15.8 us (3%)
    reduce_scatter x1, waiting for transfers between devices, per_device(): lax.psum_scatter(partial_proj, 'ga', scatter_dimension=1, tiled=True)  58.1 us
    all_to_all x4, waiting for transfers between devices, exchange(): return lax.all_to_all(piece, 'ga', split_axis=0, concat_axis=0, tiled=True)  46.6 us
    psum x1, blocking collectives, per_device(): oxygens = lax.psum(everyone, 'ga')  35 us
    unnamed x69, local copies, waits for them, and re-layouts  32.2 us
    all_to_all x4, starting transfers between devices, exchange(): return lax.all_to_all(piece, 'ga', split_axis=0, concat_axis=0, tiled=True)  31.6 us
    dot_general x4, matrix products, plane_out(): jnp.einsum('qk,bk->qb', plane_table, part[p], preferred_element_type=jnp....  25.8 us
    all_gather x1, blocking collectives, per_device(): lax.all_gather(mixed_rows.astype(jnp.bfloat16), 'ga', axis=0, tiled=True)  25.5 us
    all_to_all x1, waiting for transfers between devices, per_device(): lax.all_to_all(jnp.concatenate([packed.reshape(parts, bands // parts, ban...  16.9 us
  transfers between devices with their start and end apart: 7, of which 6 were waited for; matrix products, arithmetic and copies ran while one was open for 24% of the time, Pallas kernels for 0%

commit v1 on v0

--- a/solution.py
+++ b/solution.py
@@ -1,7 +1,11 @@
+import functools
+
 import jax
 import jax.numpy as jnp
 import numpy as np
 from jax import lax
+from jax.experimental import pallas as pl
+from jax.experimental.pallas import tpu as pltpu
 from jax.sharding import PartitionSpec as P
 
 BEADS = 32
@@ -341,10 +345,631 @@
     return (jnp.stack(new_waves), bead_forces)
 
 
+def product(left_mat, right_mat):
+    return jnp.dot(left_mat, right_mat, preferred_element_type=jnp.float32)
+
+
+def trig_tables():
+    small = np.arange(NGRID)
+    angle = small[:, None] * small[None, :] % NGRID * (2.0 * np.pi / NGRID)
+    cosines, sines = np.cos(angle), np.sin(angle)
+    rows = [np.repeat(cosines, NGRID, 1), np.repeat(sines, NGRID, 1)]
+    rows += [np.tile(cosines, (1, NGRID)), np.tile(sines, (1, NGRID))]
+    return jnp.asarray(np.stack(rows), jnp.float32)
+
+
+def cross_tables(parts, planes, share):
+    spot = (np.arange(parts)[None, :] * planes + np.arange(planes)[:, None]).reshape(-1)
+    angle = spot[:, None] * spot[None, :] % NGRID * (2.0 * np.pi / NGRID)
+    same = np.eye(share)
+    pair = np.stack([np.kron(np.cos(angle), same), np.kron(np.sin(angle), same)])
+    return jnp.asarray(pair.astype(np.float32), jnp.bfloat16)
+
+
+def step_kernel(
+    sizes,
+    psi_hbm,
+    own_waves,
+    grid,
+    trig,
+    cross,
+    vloc,
+    trial_hbm,
+    mixed_out,
+    force_out,
+    psi,
+    all_waves,
+    table_cos,
+    table_sin,
+    wave_cos,
+    wave_sin,
+    plane_cos,
+    plane_sin,
+    potential,
+    got,
+    middle,
+    giving,
+    back,
+    base,
+    trial,
+    partial,
+    landing,
+    gathered,
+    turned,
+    margin,
+    landing_two,
+    gathered_two,
+    force_sum,
+    force_land,
+    grid_rows,
+    local_sem,
+    wave_sems,
+    out_sems,
+    back_sems,
+    force_sems,
+    sum_sems,
+    share_sems,
+):
+    parts, bands, local_g = sizes
+    side = NGRID * NGRID
+    planes = local_g // side
+    share = bands // (parts * CHUNKS)
+    block = parts * share
+    steps = parts.bit_length() - 1
+    tile = 256
+    me = lax.axis_index("ga")
+
+    def other(turn):
+        total = 0
+        for bit in range(steps):
+            size = 1 << bit
+            total = total + (me // size + turn // size) % 2 * size
+        return total
+
+    def remote(source, target, sems, peer):
+        return pltpu.make_async_remote_copy(
+            src_ref=source,
+            dst_ref=target,
+            send_sem=sems[0],
+            recv_sem=sems[1],
+            device_id={"ga": peer},
+            device_id_type=pl.DeviceIdType.MESH,
+        )
+
+    def each_peer(act):
+        def body(turn, carry):
+            act(turn)
+            return carry
+
+        lax.fori_loop(1, parts, body, 0)
+
+    def pair(sems, *spot):
+        return sems.at[(0,) + spot], sems.at[(1,) + spot]
+
+    def wave_copy(turn):
+        waters = own_waves.shape[0]
+        spot = pl.ds(pl.multiple_of(me * waters, waters), waters)
+        return remote(own_waves, all_waves.at[spot], pair(wave_sems, turn), other(turn))
+
+    def out_copy(chunk, turn):
+        peer = other(turn)
+        source = pl.ds(pl.multiple_of(chunk * block + peer * share, share), share)
+        target = pl.ds(pl.multiple_of(me * share, share), share)
+        return remote(
+            psi_hbm.at[source], got.at[chunk, target], pair(out_sems, chunk, turn), peer
+        )
+
+    def back_copy(chunk, turn):
+        peer = other(turn)
+        source = pl.ds(pl.multiple_of(peer * share, share), share)
+        target = pl.ds(pl.multiple_of(chunk * block + me * share, share), share)
+        return remote(
+            giving.at[chunk, source], back.at[target], pair(back_sems, chunk, turn), peer
+        )
+
+    def force_copy(turn):
+        peer = other(turn)
+        waters = own_waves.shape[0]
+        source = pl.ds(pl.multiple_of(peer * waters, waters), waters)
+        return remote(
+            force_sum.at[source], force_land.at[me], pair(force_sems, turn), peer
+        )
+
+    local_psi = pltpu.make_async_copy(psi_hbm, psi, local_sem.at[0])
+    local_psi.start()
+    barrier = pltpu.get_barrier_semaphore()
+
+    def greet(turn):
+        pl.semaphore_signal(
+            barrier, inc=1, device_id={"ga": other(turn)}, device_id_type=pl.DeviceIdType.MESH
+        )
+
+    each_peer(greet)
+    pl.semaphore_wait(barrier, parts - 1)
+
+    units = [(chunk, far) for chunk in range(CHUNKS) for far in range(parts // 2)]
+    queue = list(units)
+
+    def issue(count):
+        for _ in range(count):
+            if queue:
+                chunk, far = queue.pop(0)
+                out_copy(chunk, parts // 2 + far).start()
+                if far > 0:
+                    out_copy(chunk, far).start()
+
+    each_peer(lambda turn: wave_copy(turn).start())
+    issue(2)
+
+    waters = own_waves.shape[0]
+    own_spot = pl.ds(pl.multiple_of(me * waters, waters), waters)
+    all_waves[own_spot, :] = own_waves[...]
+    grid_rows[...] = jnp.zeros_like(grid_rows)
+    grid_rows[: grid.shape[0], :] = grid[...]
+
+    def plane_rows(row, carry):
+        spot = pl.ds(pl.multiple_of(row * NGRID, NGRID), NGRID)
+        across_cos, across_sin = trig[0, pl.ds(row, 1), :], trig[1, pl.ds(row, 1), :]
+        plane_cos[spot, :] = (across_cos * trig[2] - across_sin * trig[3]).astype(jnp.bfloat16)
+        plane_sin[spot, :] = (across_sin * trig[2] + across_cos * trig[3]).astype(jnp.bfloat16)
+        return carry
+
+    lax.fori_loop(0, NGRID, plane_rows, 0)
+
+    def potential_rows(spot, carry):
+        plane = spot % planes * parts + spot // planes
+        rows = pl.ds(pl.multiple_of(plane * share, share), share)
+        value = vloc[pl.ds(spot, 1), :] * (1.0 / NGRID**3)
+        potential[rows, :] = jnp.broadcast_to(value, (share, side))
+        return carry
+
+    lax.fori_loop(0, NGRID, potential_rows, 0)
+
+    each_peer(lambda turn: wave_copy(turn).wait_recv())
+    lane = lax.broadcasted_iota(jnp.int32, all_waves.shape, 1)
+    line = lax.broadcasted_iota(jnp.int32, (all_waves.shape[1], tile), 0)
+    place = lax.broadcasted_iota(jnp.int32, (all_waves.shape[1], tile), 1)
+
+    def pick(first, spot):
+        return jnp.where(line == first * NGRID + spot, 1.0, 0.0)
+
+    def spread(first, spot):
+        return lax.dot_general(
+            all_waves[...],
+            pick(first, spot),
+            (((1,), (0,)), ((), ())),
+            precision=highest,
+            preferred_element_type=jnp.float32,
+        )
+
+    def table_tile(step, carry):
+        first = step * tile
+        flat = first + place
+        rise, along = flat // NGRID, flat % NGRID
+        rise_cos, rise_sin = spread(2, rise), spread(3, rise)
+        long_cos, long_sin = spread(4, along), spread(5, along)
+        flat_cos = rise_cos * long_cos - rise_sin * long_sin
+        flat_sin = rise_sin * long_cos + rise_cos * long_sin
+        for plane in range(planes):
+            level = me * planes + plane
+            c = jnp.sum(jnp.where(lane == level, all_waves[...], 0.0), axis=1, keepdims=True)
+            s = jnp.sum(
+                jnp.where(lane == level + NGRID, all_waves[...], 0.0), axis=1, keepdims=True
+            )
+            spot = pl.ds(pl.multiple_of(plane * side + first, tile), tile)
+            profile = grid[0:1, spot]
+            full_cos = profile * (c * flat_cos - s * flat_sin)
+            full_sin = profile * (s * flat_cos + c * flat_sin)
+            wave_cos[:, spot] = full_cos
+            wave_sin[:, spot] = full_sin
+            table_cos[:, spot] = full_cos.astype(jnp.bfloat16)
+            table_sin[:, spot] = full_sin.astype(jnp.bfloat16)
+        return carry
+
+    lax.fori_loop(0, side // tile, table_tile, 0)
+    local_psi.wait()
+    partial[...] = jnp.zeros_like(partial)
+
+    def project(step, carry):
+        spot = pl.ds(pl.multiple_of(step * tile, tile), tile)
+        far = pl.ds(pl.multiple_of(local_g + step * tile, tile), tile)
+        real, imag = psi[:, spot], psi[:, far]
+        cosines, sines = table_cos[:, spot], table_sin[:, spot]
+        partial[:WATERS, :] += inner(cosines, real) - inner(sines, imag)
+        partial[WATERS:, :] += inner(sines, real) + inner(cosines, imag)
+        return carry
+
+    lax.fori_loop(0, local_g // tile, project, 0)
+
+    def own_start(upto, rows):
+        start = 0
+        for bit in range(upto):
+            start = start + me // (1 << bit) % 2 * (rows >> (bit + 1))
+        return start
+
+    def sum_step(values, land, which, bit, between):
+        rows = values.shape[0]
+        half = rows >> (bit + 1)
+        size = 1 << bit
+        mine = me // size % 2
+        start = own_start(bit, rows)
+        away = pl.ds(pl.multiple_of(start + (1 - mine) * half, half), half)
+        keep = pl.ds(pl.multiple_of(start + mine * half, half), half)
+        spot = pl.ds(rows - 2 * half, half)
+        copy = remote(
+            values.at[away], land.at[spot], pair(sum_sems, which, bit), me + (1 - 2 * mine) * size
+        )
+        copy.start()
+        between()
+        copy.wait()
+        values[keep, :] += land[spot, :]
+
+    def share_step(values, which, bit, between):
+        rows = values.shape[0]
+        size = 1 << bit
+        mine = me // size % 2
+        count = rows >> (bit + 1)
+        spot = pl.ds(pl.multiple_of(own_start(bit + 1, rows), count), count)
+        copy = remote(
+            values.at[spot],
+            values.at[spot],
+            pair(share_sems, which, bit),
+            me + (1 - 2 * mine) * size,
+        )
+        copy.start()
+        between()
+        copy.wait()
+
+    for bit in range(steps):
+        sum_step(partial, landing, 0, bit, lambda: issue(1))
+    own_rows = partial.shape[0] // parts
+    own = pl.ds(pl.multiple_of(own_start(steps, partial.shape[0]), own_rows), own_rows)
+    gathered[own, :] = (partial[own, :] * (1.0 / GVECS)).astype(jnp.bfloat16)
+    for bit in reversed(range(steps)):
+        share_step(gathered, 0, bit, lambda: issue(1))
+    issue(len(units))
+
+    for first in range(0, gathered.shape[0], tile):
+        for second in range(0, bands, tile):
+            part = gathered[first : first + tile, second : second + tile].astype(jnp.float32)
+            turned[second : second + tile, first : first + tile] = part.T.astype(jnp.bfloat16)
+
+    def transform(chunk):
+        mine = pl.ds(pl.multiple_of(me * share, share), share)
+        own_bands = pl.ds(pl.multiple_of(chunk * block + me * share, share), share)
+        got[chunk, mine, :] = psi[own_bands, :]
+        each_peer(lambda turn: out_copy(chunk, turn).wait_recv())
+        columns = side // tile
+
+        def forward(step, carry):
+            plane, column = step // columns, step % columns
+            spot = pl.ds(pl.multiple_of(column * tile, tile), tile)
+            rows = pl.ds(pl.multiple_of(plane * block, block), block)
+            real = got[chunk, :, pl.ds(pl.multiple_of(plane * side, side), side)]
+            imag = got[chunk, :, pl.ds(pl.multiple_of(local_g + plane * side, side), side)]
+            cosines, sines = plane_cos[:, spot], plane_sin[:, spot]
+            middle[0, rows, spot] = (product(real, cosines) - product(imag, sines)).astype(
+                jnp.bfloat16
+            )
+            middle[1, rows, spot] = (product(real, sines) + product(imag, cosines)).astype(
+                jnp.bfloat16
+            )
+            return carry
+
+        lax.fori_loop(0, planes * columns, forward, 0)
+
+        def lines(column, carry):
+            spot = pl.ds(pl.multiple_of(column * tile, tile), tile)
+            real, imag = middle[0, :, spot], middle[1, :, spot]
+            value = potential[:, spot]
+            cosines, sines = cross[0], cross[1]
+            upper = (product(cosines, real) - product(sines, imag)) * value
+            lower = (product(sines, real) + product(cosines, imag)) * value
+            upper, lower = upper.astype(jnp.bfloat16), lower.astype(jnp.bfloat16)
+            middle[0, :, spot] = (product(cosines, upper) + product(sines, lower)).astype(
+                jnp.bfloat16
+            )
+            middle[1, :, spot] = (product(cosines, lower) - product(sines, upper)).astype(
+                jnp.bfloat16
+            )
+            return carry
+
+        lax.fori_loop(0, columns, lines, 0)
+
+        def backward(step, carry):
+            plane, column = step // columns, step % columns
+            spot = pl.ds(pl.multiple_of(column * tile, tile), tile)
+            rows = pl.ds(pl.multiple_of(plane * block, block), block)
+            real, imag = middle[0, rows, :], middle[1, rows, :]
+            cosines, sines = plane_cos[:, spot], plane_sin[:, spot]
+            upper = pl.ds(pl.multiple_of(plane * side + column * tile, tile), tile)
+            lower = pl.ds(pl.multiple_of(local_g + plane * side + column * tile, tile), tile)
+            giving[chunk, :, upper] = (product(real, cosines) + product(imag, sines)).astype(
+                jnp.bfloat16
+            )
+            giving[chunk, :, lower] = (product(imag, cosines) - product(real, sines)).astype(
+                jnp.bfloat16
+            )
+            return carry
+
+        lax.fori_loop(0, planes * columns, backward, 0)
+        back[own_bands, :] = giving[chunk, mine, :]
+        for far in range(parts // 2):
+            back_copy(chunk, parts // 2 + far).start()
+            if far > 0:
+                back_copy(chunk, far).start()
+
+    transform(0)
+
+    force_sum[...] = jnp.zeros_like(force_sum)
+
+    def local_part(step, carry):
+        spot = pl.ds(pl.multiple_of(step * tile, tile), tile)
+        far = pl.ds(pl.multiple_of(local_g + step * tile, tile), tile)
+        kinetic = 1.0 - step_size * grid[1:2, spot]
+        real, imag = psi[:, spot], psi[:, far]
+        cosines, sines = table_cos[:, spot], table_sin[:, spot]
+        turned_re, turned_im = turned[:, :WATERS], turned[:, WATERS:]
+        strength = step_size * nonlocal_strength
+        base[:, spot] = kinetic * real.astype(jnp.float32) - strength * (
+            product(turned_re, cosines) + product(turned_im, sines)
+        )
+        base[:, far] = kinetic * imag.astype(jnp.float32) - strength * (
+            product(turned_im, cosines) - product(turned_re, sines)
+        )
+        proj_re, proj_im = gathered[:WATERS, :], gathered[WATERS:, :]
+        weighted_re = product(proj_re, real) + product(proj_im, imag)
+        weighted_im = product(proj_re, imag) - product(proj_im, real)
+        mixed = wave_cos[:, spot] * weighted_im + wave_sin[:, spot] * weighted_re
+        force_sum[...] += lax.dot_general(
+            mixed,
+            grid_rows[:, spot],
+            (((1,), (1,)), ((), ())),
+            precision=highest,
+            preferred_element_type=jnp.float32,
+        )
+        return carry
+
+    lax.fori_loop(0, local_g // tile, local_part, 0)
+    force_land[me] = force_sum[own_spot, :]
+    each_peer(lambda turn: force_copy(turn).start())
+
+    transform(1)
+
+    def finish(chunk):
+        def rows_of(turn, carry):
+            @pl.when(turn > 0)
+            def _():
+                back_copy(chunk, turn).wait_recv()
+
+            rows = pl.ds(
+                pl.multiple_of(chunk * block + other(turn) * share, share), share
+            )
+            value = base[rows, :] - step_size * back[rows, :].astype(jnp.float32)
+            value = value.astype(jnp.bfloat16)
+            trial[0, rows, :] = value[:, :local_g]
+            trial[1, rows, :] = value[:, local_g:]
+            return carry
+
+        lax.fori_loop(0, parts, rows_of, 0)
+
+    corner_row = lax.broadcasted_iota(jnp.int32, (block, block), 0)
+    corner_column = lax.broadcasted_iota(jnp.int32, (block, block), 1)
+
+    def overlap(first, second):
+        rows = pl.ds(first * block, block)
+        columns = pl.ds(second * block, block)
+
+        def even(spot):
+            return inner(trial[0, rows, spot], trial[0, columns, spot]) + inner(
+                trial[1, rows, spot], trial[1, columns, spot]
+            )
+
+        def odd(spot):
+            return inner(trial[1, rows, spot], trial[0, columns, spot]) - inner(
+                trial[0, rows, spot], trial[1, columns, spot]
+            )
+
+        margin[rows, columns] = jnp.zeros((block, block), jnp.float32)
+
+        def add(step, carry):
+            spot = pl.ds(pl.multiple_of(step * tile, tile), tile)
+            if first < second:
+                value = even(spot)
+            elif first > second:
+                value = odd(spot)
+            else:
+                value = jnp.where(corner_row <= corner_column, even(spot), odd(spot))
+            margin[rows, columns] += value
+            return carry
+
+        lax.fori_loop(0, local_g // tile, add, 0)
+
+    for chunk in range(CHUNKS):
+        finish(chunk)
+        trial_copy = pltpu.make_async_copy(
+            trial.at[:, pl.ds(chunk * block, block)],
+            trial_hbm.at[:, pl.ds(chunk * block, block)],
+            local_sem.at[1 + chunk],
+        )
+        trial_copy.start()
+        for first in range(chunk + 1):
+            overlap(first, chunk)
+            if first != chunk:
+                overlap(chunk, first)
+
+    for bit in range(steps):
+        sum_step(margin, landing_two, 1, bit, lambda: None)
+    start = own_start(steps, bands)
+    own_rows = bands // parts
+    own = pl.ds(pl.multiple_of(start, own_rows), own_rows)
+    row = start + lax.broadcasted_iota(jnp.int32, (own_rows, bands), 0)
+    column = lax.broadcasted_iota(jnp.int32, (own_rows, bands), 1)
+    mixed_rows = jnp.where(row == column, 1.5, 0.0) - (0.5 / GVECS) * margin[own, :]
+    gathered_two[own, :] = mixed_rows.astype(jnp.bfloat16)
+    for bit in reversed(range(steps)):
+        share_step(gathered_two, 1, bit, lambda: None)
+
+    for first in range(0, bands, tile):
+        for second in range(0, bands, tile):
+            there = gathered_two[first : first + tile, second : second + tile]
+            flipped = gathered_two[second : second + tile, first : first + tile]
+            there = there.astype(jnp.float32)
+            flipped = flipped.astype(jnp.float32).T
+            row = first + lax.broadcasted_iota(jnp.int32, (tile, tile), 0)
+            column = second + lax.broadcasted_iota(jnp.int32, (tile, tile), 1)
+            mix_re = jnp.where(row <= column, there, flipped)
+            mix_im = jnp.where(
+                row > column, there, jnp.where(row < column, -flipped, jnp.zeros_like(there))
+            )
+            mixed_out[0, first : first + tile, second : second + tile] = mix_re.astype(
+                jnp.bfloat16
+            )
+            mixed_out[1, first : first + tile, second : second + tile] = mix_im.astype(
+                jnp.bfloat16
+            )
+
+    each_peer(lambda turn: force_copy(turn).wait_recv())
+
+    def add_force(source, carry):
+        return carry + force_land[source]
+
+    force_out[...] = lax.fori_loop(0, parts, add_force, jnp.zeros(force_out.shape, jnp.float32))
+    for chunk in range(CHUNKS):
+        pltpu.make_async_copy(
+            trial.at[:, pl.ds(chunk * block, block)],
+            trial_hbm.at[:, pl.ds(chunk * block, block)],
+            local_sem.at[1 + chunk],
+        ).wait()
+        each_peer(lambda turn: out_copy(chunk, turn).wait_send())
+        each_peer(lambda turn: back_copy(chunk, turn).wait_send())
+    each_peer(lambda turn: wave_copy(turn).wait_send())
+    each_peer(lambda turn: force_copy(turn).wait_send())
+
+
+def fused_device(positions, weights, psi, vloc):
+    near_forces = field_forces(positions)
+    weight_float = weights.astype(jnp.float32)
+    mixing = weight_float / jnp.sum(weight_float, axis=1, keepdims=True)
+    parts = lax.axis_size("ga")
+    bands, local_g = psi.shape[1], psi.shape[3]
+    side = NGRID * NGRID
+    planes = local_g // side
+    share = bands // (parts * CHUNKS)
+    block = parts * share
+    waters = positions.shape[2] // 3
+    near_oxygen = jnp.einsum("cj,jan->can", mixing, positions[:, :, 0::3], precision=highest)[0]
+    spokes = frequency(jnp.arange(NGRID, dtype=jnp.int32), NGRID)
+    angles = near_oxygen.T[:, :, None] * spokes
+    own_waves = jnp.stack([jnp.cos(angles), jnp.sin(angles)], 2).reshape(waters, 6 * NGRID)
+    own_waves = jnp.pad(own_waves, ((0, 0), (0, 2 * NGRID)))
+    flat_index = lax.axis_index("ga") * local_g + jnp.arange(local_g, dtype=jnp.int32)
+    gvectors = [
+        frequency(flat_index // side, NGRID),
+        frequency(flat_index // NGRID % NGRID, NGRID),
+        frequency(flat_index % NGRID, NGRID),
+    ]
+    square = gvectors[0] * gvectors[0] + gvectors[1] * gvectors[1] + gvectors[2] * gvectors[2]
+    profile = jnp.exp(-0.5 * width_square * square)
+    nothing = jnp.zeros_like(square)
+    grid = jnp.stack([profile, 0.5 * square] + gvectors + [nothing] * 3)
+    vmem = pl.BlockSpec(memory_space=pltpu.VMEM)
+    anywhere = pl.BlockSpec(memory_space=pl.ANY)
+    steps = parts.bit_length() - 1
+    f32, bf16 = jnp.float32, jnp.bfloat16
+    dma = pltpu.SemaphoreType.DMA
+    trial, mixed, force = pl.pallas_call(
+        functools.partial(step_kernel, (parts, bands, local_g)),
+        out_shape=(
+            jax.ShapeDtypeStruct((2, bands, local_g), bf16),
+            jax.ShapeDtypeStruct((2, bands, bands), bf16),
+            jax.ShapeDtypeStruct((waters, 128), f32),
+        ),
+        in_specs=[anywhere, vmem, vmem, vmem, vmem, vmem],
+        out_specs=(anywhere, vmem, vmem),
+        scratch_shapes=[
+            pltpu.VMEM((bands, 2 * local_g), bf16),
+            pltpu.VMEM((WATERS, 8 * NGRID), f32),
+            pltpu.VMEM((WATERS, local_g), bf16),
+            pltpu.VMEM((WATERS, local_g), bf16),
+            pltpu.VMEM((WATERS, local_g), f32),
+            pltpu.VMEM((WATERS, local_g), f32),
+            pltpu.VMEM((side, side), bf16),
+            pltpu.VMEM((side, side), bf16),
+            pltpu.VMEM((planes * block, side), f32),
+            pltpu.VMEM((CHUNKS, block, 2 * local_g), bf16),
+            pltpu.VMEM((2, planes * block, side), bf16),
+            pltpu.VMEM((CHUNKS, block, 2 * local_g), bf16),
+            pltpu.VMEM((bands, 2 * local_g), bf16),
+            pltpu.VMEM((bands, 2 * local_g), f32),
+            pltpu.VMEM((2, bands, local_g), bf16),
+            pltpu.VMEM((2 * WATERS, bands), f32),
+            pltpu.VMEM((2 * WATERS, bands), f32),
+            pltpu.VMEM((2 * WATERS, bands), bf16),
+            pltpu.VMEM((bands, 2 * WATERS), bf16),
+            pltpu.VMEM((bands, bands), f32),
+            pltpu.VMEM((bands, bands), f32),
+            pltpu.VMEM((bands, bands), bf16),
+            pltpu.VMEM((WATERS, 128), f32),
+            pltpu.VMEM((parts, waters, 128), f32),
+            pltpu.VMEM((128, local_g), f32),
+            dma((1 + CHUNKS,)),
+            dma((2, parts)),
+            dma((2, CHUNKS, parts)),
+            dma((2, CHUNKS, parts)),
+            dma((2, parts)),
+            dma((2, 2, steps)),
+            dma((2, 2, steps)),
+        ],
+        compiler_params=pltpu.CompilerParams(
+            collective_id=0, has_side_effects=True, vmem_limit_bytes=67043328
+        ),
+    )(
+        psi[0].reshape(bands, 2 * local_g),
+        own_waves,
+        grid,
+        trig_tables(),
+        cross_tables(parts, planes, share),
+        vloc[0].reshape(NGRID, side),
+    )
+    turn = jnp.concatenate(
+        [
+            jnp.concatenate([mixed[0], -mixed[1]], 1),
+            jnp.concatenate([mixed[1], mixed[0]], 1),
+        ],
+        0,
+    )
+    updated = product(turn, trial.reshape(2 * bands, local_g)).astype(jnp.bfloat16)
+    psi_new = updated.reshape(2, bands, local_g).transpose(1, 0, 2)[None]
+    strength = 2.0 * occupation * nonlocal_strength / GVECS
+    oxygen_force = strength * force[:, 2:5].T
+    hydrogen_zero = jnp.zeros_like(oxygen_force)
+    dft_force = jnp.stack([oxygen_force, hydrogen_zero, hydrogen_zero], axis=2).reshape(1, 3, -1)
+    contracted_force = mixing[0][:, None, None] * dft_force
+    return (psi_new, near_forces + BEADS / CBEADS * contracted_force)
+
+
+def step_device(positions, weights, psi, vloc):
+    parts = lax.axis_size("ga")
+    bands, local_g = psi.shape[1], psi.shape[3]
+    side = NGRID * NGRID
+    fits = (
+        local_g % side == 0
+        and parts & (parts - 1) == 0
+        and parts >= 4
+        and bands % (parts * CHUNKS * 16) == 0
+        and bands // CHUNKS % 256 == 0
+        and bands * local_g <= 2**20
+    )
+    if fits:
+        return fused_device(positions, weights, psi, vloc)
+    return per_device(positions, weights, psi, vloc)
+
+
 def solution(mesh):
     placed = (P("rep", None, "ga"), P(), P("rep", None, None, "ga"), P("rep", None))
     return jax.shard_map(
-        per_device,
+        step_device,
         mesh=mesh,
         in_specs=placed,
         out_specs=(P("rep", None, None, "ga"), P("rep", None, "ga")),

time: 458 us -> 301 us (0.66); the launches traced: 450 us -> 300 us
  Pallas kernels: 0 us -> 253 us
  waiting for transfers between devices: 125 us -> 0 us
  matrix products: 87.9 us -> 14.9 us
  blocking collectives: 60.5 us -> 0 us
  local copies, waits for them, and re-layouts: 74.3 us -> 23.8 us
  starting transfers between devices: 47.6 us -> 0 us
  other arithmetic: 38.4 us -> 7.12 us
  between operations: 15.8 us -> 0.79 us
    pallas_call x0 -> x1, Pallas kernels: none -> 253 us  [fused_device(): pl.pallas_call(functools.partial(step_kernel, (parts, bands, local_g)), o...]
    dot_general x22 -> x2, matrix products: 87.9 us -> 14.9 us  [the longest x1 13.4 us: product(): return jnp.dot(left_mat, right_mat, preferred_element_type=jnp.float32)]
    all_to_all x6 -> x0, waiting for transfers between devices: 67.2 us -> none  [the longest x4 46.6 us: exchange(): return lax.all_to_all(piece, 'ga', split_axis=0, concat_axis=0, tiled=True)]
    reduce_scatter x1 -> x0, waiting for transfers between devices: 58.1 us -> none  [per_device(): lax.psum_scatter(partial_proj, 'ga', scatter_dimension=1, tiled=True)]
    all_to_all x6 -> x0, starting transfers between devices: 47.1 us -> none  [the longest x4 31.6 us: exchange(): return lax.all_to_all(piece, 'ga', split_axis=0, concat_axis=0, tiled=True)]
    psum x1 -> x0, blocking collectives: 35 us -> none  [per_device(): oxygens = lax.psum(everyone, 'ga')]
    all_gather x1 -> x0, blocking collectives: 25.5 us -> none  [per_device(): lax.all_gather(mixed_rows.astype(jnp.bfloat16), 'ga', axis=0, tiled=True)]
    unnamed x69 -> x7, local copies, waits for them, and re-layouts: 32.2 us -> 8.9 us
  transfers between devices with their start and end apart: 7 -> 0, of which waited for: 6 -> 0; matrix products, arithmetic and copies ran while one was open for 24% -> 0% of each run, Pallas kernels for 0% -> 0%
where the time goes in v1:
time: 301 us; the launch traced here: 300 us
  Pallas kernels  253 us (84%)
  local copies, waits for them, and re-layouts  23.8 us (8%)
  matrix products  14.9 us (5%)
  other arithmetic  7.12 us (2%)
    pallas_call x1, Pallas kernels, fused_device(): pl.pallas_call(functools.partial(step_kernel, (parts, bands, local_g)), o...  253 us
    dot_general x1, matrix products, product(): return jnp.dot(left_mat, right_mat, preferred_element_type=jnp.float32)  13.4 us
    unnamed x7, local copies, waits for them, and re-layouts  8.9 us
    reshape x1, local copies, waits for them, and re-layouts, fused_device(): psi_new = updated.reshape(2, bands, local_g).transpose(1, 0, 2)[None]  6.33 us

profile of v1, /device:TPU:0, one launch (start us, length us, event | category | flops | bytes accessed | tf_op | source)
XLA Modules:
  0.0 299.9 jit_solution(3779789035967650957)
XLA Ops:
  0.6 1.1 slice.37
  1.7 1.1 slice.40
  2.8 1.1 slice.41
  3.9 0.1 copy.23
  4.1 0.7 reshape.283
  4.7 0.1 fusion.13
  4.9 0.2 fusion.17
  5.0 0.2 broadcast_multiply_fusion
  5.2 0.7 stack.37.grid
  6.0 1.3 convert_reduce_fusion
  7.2 1.4 fusion.24
  8.7 0.2 multiply_cosine_fusion
  8.9 0.1 reshape.280
  9.0 0.6 pad.5.own_waves
  9.6 0.0 copy-start
  9.6 6.6 %copy.34 = bf16[64,8,2,2048]{3,1,2,0:T(8,128)(2,1)} copy(bf16[64,8,2,2048]{3,2,1,0:T(2,128)(2,1)} %bitcast.41) | data formatting | bytes 8388608
  16.2 0.6 broadcast.662
  16.8 0.0 copy-done
  16.8 1.0 reduce.4
  17.8 0.7 reshape_squeeze.7.vloc
  18.5 253.3 %shard_map.77 = (bf16[2,512,2048]{2,1,0:T(8,128)(2,1)}, bf16[2,512,512]{2,1,0:T(8,128)(2,1)}, f32[16,128]{1,0:T(8,128)}) custom-call(bf16[512,4096]{1,0:T(8,128)(2,1)} %bitcast.40, f32[16,256]{1,0:T(8,128)} %pad.5.own_waves, f32[8,2048]{1,0:T(8,128)} %stack.37.grid, f32[4,32,1024]{2,1,0:T(8,128)} %constant.90.clone.trig, ...), custom_call_target="tpu_custom_call" | custom-call | tf_op jit(solution)/shard_map/pallas_call | solution.py:881
  271.8 0.8 multiply_bitcast_fusion
  272.5 0.1 copy.29
  272.6 0.1 copy.33
  272.7 0.1 mul.263
  272.8 0.9 copy.24
  273.7 0.1 fusion.29
  273.8 0.7 fusion.30
  274.5 0.1 copy.26
  274.6 0.1 copy.28
  274.7 1.3 fusion.27
  276.0 1.0 fusion.10
  277.0 0.7 copy.31
  277.7 1.3 slice_bitcast_fusion
  279.0 1.1 fusion.28
  280.1 13.4 %convolution_convert_fusion = bf16[1024,2048]{1,0:T(8,128)(2,1)S(1)} fusion(bf16[1024,2048]{1,0:T(8,128)(2,1)} %bitcast.46, bf16[512,512]{1,0:T(8,128)(2,1)S(1)} %get-tuple-element.17, bf16[512,512]{1,0:T(8,128)(2,1)S(1)} %get-tuple-element.16, bf16[512,512]{1,0:T(8,128)(2,1)S(1)} %fusion.28), kind=kOutput, calls=%fused_computation.1 | convolution fusion | flops 4305453056 | bytes 9961472 | tf_op jit(solution)/shard_map/dot_general | solution.py:349
  293.5 6.3 %copy.37 = bf16[2,512,2048]{2,0,1:T(2,128)(2,1)} copy(bf16[2,512,2048]{2,1,0:T(8,128)(2,1)S(1)} %bitcast.43) | data formatting | bytes 8388608 | tf_op jit(solution)/shard_map/reshape | solution.py:943
  (11 shorter events, 0.1 us)
Async XLA Ops:
  9.6 7.2 %copy-start = (f32[1,32768]{1,0:T(1,128)S(1)}, f32[1,32768]{1,0:T(1,128)}, u32[]{:S(2)}) copy-start(f32[1,32768]{1,0:T(1,128)} %param.9) | copy-start | bytes 393220

commit v2 on v1

--- a/solution.py
+++ b/solution.py
@@ -369,15 +369,19 @@
 def step_kernel(
     sizes,
     psi_hbm,
-    own_waves,
-    grid,
+    positions,
+    weights,
     trig,
     cross,
     vloc,
     trial_hbm,
     mixed_out,
     force_out,
+    raw,
     psi,
+    own_waves,
+    grid,
+    near,
     all_waves,
     table_cos,
     table_sin,
@@ -387,6 +391,7 @@
     plane_sin,
     potential,
     got,
+    whole,
     middle,
     giving,
     back,
@@ -475,7 +480,7 @@
             force_sum.at[source], force_land.at[me], pair(force_sems, turn), peer
         )
 
-    local_psi = pltpu.make_async_copy(psi_hbm, psi, local_sem.at[0])
+    local_psi = pltpu.make_async_copy(psi_hbm, raw, local_sem.at[0])
     local_psi.start()
     barrier = pltpu.get_barrier_semaphore()
 
@@ -485,6 +490,36 @@
         )
 
     each_peer(greet)
+    waters = own_waves.shape[0]
+    atoms = positions.shape[2]
+    beads = positions.shape[0]
+
+    def exact(left_mat, right_mat, right_axis=0):
+        return lax.dot_general(
+            left_mat,
+            right_mat,
+            (((1,), (right_axis,)), ((), ())),
+            precision=highest,
+            preferred_element_type=jnp.float32,
+        )
+
+    def spots(shape):
+        return lax.broadcasted_iota(jnp.int32, shape, 0), lax.broadcasted_iota(jnp.int32, shape, 1)
+
+    weight_row = weights[...].astype(jnp.float32)
+    mixing = weight_row / jnp.sum(weight_row, axis=1, keepdims=True)
+    wave_row, wave_lane = spots(own_waves.shape)
+    own_row, own_atom = spots((waters, atoms))
+    oxygen_pick = jnp.where(own_atom == 3 * own_row, 1.0, 0.0)
+    spokes = frequency(wave_lane % NGRID, NGRID)
+    angles = jnp.zeros(own_waves.shape, jnp.float32)
+    for axis in range(3):
+        centre = exact(jnp.broadcast_to(mixing, (8, beads)), positions[:, axis, :])
+        column = exact(oxygen_pick, centre, 1)[:, 0:1]
+        angles += column * jnp.where(wave_lane // (2 * NGRID) == axis, spokes, 0.0)
+    own_waves[...] = jnp.where(wave_lane // NGRID % 2 == 0, jnp.cos(angles), jnp.sin(angles))
+    own_spot = pl.ds(pl.multiple_of(me * waters, waters), waters)
+    all_waves[own_spot, :] = own_waves[...]
     pl.semaphore_wait(barrier, parts - 1)
 
     units = [(chunk, far) for chunk in range(CHUNKS) for far in range(parts // 2)]
@@ -501,11 +536,18 @@
     each_peer(lambda turn: wave_copy(turn).start())
     issue(2)
 
-    waters = own_waves.shape[0]
-    own_spot = pl.ds(pl.multiple_of(me * waters, waters), waters)
-    all_waves[own_spot, :] = own_waves[...]
+    flat_index = me * local_g + lax.broadcasted_iota(jnp.int32, (1, local_g), 1)
+    gvectors = [
+        frequency(flat_index // side, NGRID),
+        frequency(flat_index // NGRID % NGRID, NGRID),
+        frequency(flat_index % NGRID, NGRID),
+    ]
+    square = gvectors[0] * gvectors[0] + gvectors[1] * gvectors[1] + gvectors[2] * gvectors[2]
+    grid[0:1, :] = jnp.exp(-0.5 * width_square * square)
+    grid[1:2, :] = 0.5 * square
     grid_rows[...] = jnp.zeros_like(grid_rows)
-    grid_rows[: grid.shape[0], :] = grid[...]
+    for axis in range(3):
+        grid_rows[axis : axis + 1, :] = gvectors[axis]
 
     def plane_rows(row, carry):
         spot = pl.ds(pl.multiple_of(row * NGRID, NGRID), NGRID)
@@ -519,12 +561,22 @@
     def potential_rows(spot, carry):
         plane = spot % planes * parts + spot // planes
         rows = pl.ds(pl.multiple_of(plane * share, share), share)
-        value = vloc[pl.ds(spot, 1), :] * (1.0 / NGRID**3)
+        value = vloc[:, pl.ds(pl.multiple_of(spot * side, side), side)] * (1.0 / NGRID**3)
         potential[rows, :] = jnp.broadcast_to(value, (share, side))
         return carry
 
     lax.fori_loop(0, NGRID, potential_rows, 0)
 
+    strip = 16
+
+    def unpack_rows(step, carry):
+        rows = pl.ds(pl.multiple_of(step * strip, strip), strip)
+        psi[rows, :local_g] = raw[rows, 0, :]
+        psi[rows, local_g:] = raw[rows, 1, :]
+        return carry
+
+    local_psi.wait()
+    lax.fori_loop(0, bands // strip, unpack_rows, 0)
     each_peer(lambda turn: wave_copy(turn).wait_recv())
     lane = lax.broadcasted_iota(jnp.int32, all_waves.shape, 1)
     line = lax.broadcasted_iota(jnp.int32, (all_waves.shape[1], tile), 0)
@@ -567,7 +619,6 @@
         return carry
 
     lax.fori_loop(0, side // tile, table_tile, 0)
-    local_psi.wait()
     partial[...] = jnp.zeros_like(partial)
 
     def project(step, carry):
@@ -637,16 +688,23 @@
     def transform(chunk):
         mine = pl.ds(pl.multiple_of(me * share, share), share)
         own_bands = pl.ds(pl.multiple_of(chunk * block + me * share, share), share)
-        got[chunk, mine, :] = psi[own_bands, :]
-        each_peer(lambda turn: out_copy(chunk, turn).wait_recv())
+        whole[mine, :] = psi[own_bands, :]
+
+        def unpack_peer(turn):
+            out_copy(chunk, turn).wait_recv()
+            rows = pl.ds(pl.multiple_of(other(turn) * share, share), share)
+            whole[rows, :local_g] = got[chunk, rows, 0, :]
+            whole[rows, local_g:] = got[chunk, rows, 1, :]
+
+        each_peer(unpack_peer)
         columns = side // tile
 
         def forward(step, carry):
             plane, column = step // columns, step % columns
             spot = pl.ds(pl.multiple_of(column * tile, tile), tile)
             rows = pl.ds(pl.multiple_of(plane * block, block), block)
-            real = got[chunk, :, pl.ds(pl.multiple_of(plane * side, side), side)]
-            imag = got[chunk, :, pl.ds(pl.multiple_of(local_g + plane * side, side), side)]
+            real = whole[:, pl.ds(pl.multiple_of(plane * side, side), side)]
+            imag = whole[:, pl.ds(pl.multiple_of(local_g + plane * side, side), side)]
             cosines, sines = plane_cos[:, spot], plane_sin[:, spot]
             middle[0, rows, spot] = (product(real, cosines) - product(imag, sines)).astype(
                 jnp.bfloat16
@@ -699,6 +757,26 @@
             if far > 0:
                 back_copy(chunk, far).start()
 
+    def near_forces():
+        here, there = spots((atoms, atoms))
+        same = jnp.where(here == there, 1.0, 0.0)
+        offset_pick = same - jnp.where(here == there - there % 3, 1.0, 0.0)
+        pull_pick = same - jnp.where(there == here - here % 3, 1.0, 0.0)
+        bead, beside = spots((beads, beads))
+        spring = 2.0 * jnp.where(bead == beside, 1.0, 0.0)
+        spring -= jnp.where((bead + 1) % beads == beside, 1.0, 0.0)
+        spring -= jnp.where((beside + 1) % beads == bead, 1.0, 0.0)
+        offsets = [exact(positions[:, axis, :], offset_pick) for axis in range(3)]
+        squares = offsets[0] * offsets[0] + offsets[1] * offsets[1] + offsets[2] * offsets[2]
+        hydrogen = lax.broadcasted_iota(jnp.int32, squares.shape, 1) % 3 > 0
+        length = jnp.sqrt(jnp.where(hydrogen, squares, 1.0))
+        for axis in range(3):
+            pull = -bond_stiff * (length - bond_rest) * offsets[axis] / length
+            pull = jnp.where(hydrogen, pull, 0.0)
+            near[axis] = exact(pull, pull_pick) - spring_stiff * exact(
+                spring, positions[:, axis, :]
+            )
+
     transform(0)
 
     force_sum[...] = jnp.zeros_like(force_sum)
@@ -734,7 +812,27 @@
     force_land[me] = force_sum[own_spot, :]
     each_peer(lambda turn: force_copy(turn).start())
 
+    near_forces()
     transform(1)
+    each_peer(lambda turn: force_copy(turn).wait_recv())
+
+    def add_force(source, carry):
+        return carry + force_land[source]
+
+    strength = 2.0 * occupation * nonlocal_strength / GVECS
+    total = strength * lax.fori_loop(
+        0, parts, add_force, jnp.zeros(force_land.shape[1:], jnp.float32)
+    )
+    bead_row, bead_column = spots((beads, beads))
+    mixing_column = jnp.sum(
+        jnp.where(bead_row == bead_column, jnp.broadcast_to(mixing, (beads, beads)), 0.0),
+        axis=1,
+        keepdims=True,
+    )
+    for axis in range(3):
+        placed = jnp.where(own_atom == 3 * own_row, total[:, axis : axis + 1], 0.0)
+        placed = jnp.sum(placed, axis=0, keepdims=True)
+        force_out[:, axis, :] = near[axis] + BEADS / CBEADS * (mixing_column * placed)
 
     def finish(chunk):
         def rows_of(turn, carry):
@@ -829,12 +927,6 @@
                 jnp.bfloat16
             )
 
-    each_peer(lambda turn: force_copy(turn).wait_recv())
-
-    def add_force(source, carry):
-        return carry + force_land[source]
-
-    force_out[...] = lax.fori_loop(0, parts, add_force, jnp.zeros(force_out.shape, jnp.float32))
     for chunk in range(CHUNKS):
         pltpu.make_async_copy(
             trial.at[:, pl.ds(chunk * block, block)],
@@ -847,10 +939,49 @@
     each_peer(lambda turn: force_copy(turn).wait_send())
 
 
+def rotate_kernel(sizes, mixed, trial_hbm, out, trial, sem):
+    rows, local_g = sizes
+    tile = 256
+    copy = pltpu.make_async_copy(trial_hbm, trial, sem.at[0])
+
+    @pl.when(pl.program_id(0) == 0)
+    def _():
+        copy.start()
+        copy.wait()
+
+    mix_re, mix_im = mixed[0], mixed[1]
+
+    def columns(step, carry):
+        spot = pl.ds(pl.multiple_of(step * tile, tile), tile)
+        real, imag = trial[0, :, spot], trial[1, :, spot]
+        out[:, 0, spot] = (product(mix_re, real) - product(mix_im, imag)).astype(out.dtype)
+        out[:, 1, spot] = (product(mix_im, real) + product(mix_re, imag)).astype(out.dtype)
+        return carry
+
+    lax.fori_loop(0, local_g // tile, columns, 0)
+
+
+def rotate(mixed, trial):
+    bands, local_g = trial.shape[1:]
+    rows = 128
+    return pl.pallas_call(
+        functools.partial(rotate_kernel, (rows, local_g)),
+        grid=(bands // rows,),
+        out_shape=jax.ShapeDtypeStruct((bands, 2, local_g), jnp.bfloat16),
+        in_specs=[
+            pl.BlockSpec((2, rows, bands), lambda step: (0, step, 0)),
+            pl.BlockSpec(memory_space=pl.ANY),
+        ],
+        out_specs=pl.BlockSpec((rows, 2, local_g), lambda step: (step, 0, 0)),
+        scratch_shapes=[
+            pltpu.VMEM(trial.shape, trial.dtype),
+            pltpu.SemaphoreType.DMA((1,)),
+        ],
+        compiler_params=pltpu.CompilerParams(vmem_limit_bytes=32 * 2**20),
+    )(mixed, trial)
+
+
 def fused_device(positions, weights, psi, vloc):
-    near_forces = field_forces(positions)
-    weight_float = weights.astype(jnp.float32)
-    mixing = weight_float / jnp.sum(weight_float, axis=1, keepdims=True)
     parts = lax.axis_size("ga")
     bands, local_g = psi.shape[1], psi.shape[3]
     side = NGRID * NGRID
@@ -858,21 +989,6 @@
     share = bands // (parts * CHUNKS)
     block = parts * share
     waters = positions.shape[2] // 3
-    near_oxygen = jnp.einsum("cj,jan->can", mixing, positions[:, :, 0::3], precision=highest)[0]
-    spokes = frequency(jnp.arange(NGRID, dtype=jnp.int32), NGRID)
-    angles = near_oxygen.T[:, :, None] * spokes
-    own_waves = jnp.stack([jnp.cos(angles), jnp.sin(angles)], 2).reshape(waters, 6 * NGRID)
-    own_waves = jnp.pad(own_waves, ((0, 0), (0, 2 * NGRID)))
-    flat_index = lax.axis_index("ga") * local_g + jnp.arange(local_g, dtype=jnp.int32)
-    gvectors = [
-        frequency(flat_index // side, NGRID),
-        frequency(flat_index // NGRID % NGRID, NGRID),
-        frequency(flat_index % NGRID, NGRID),
-    ]
-    square = gvectors[0] * gvectors[0] + gvectors[1] * gvectors[1] + gvectors[2] * gvectors[2]
-    profile = jnp.exp(-0.5 * width_square * square)
-    nothing = jnp.zeros_like(square)
-    grid = jnp.stack([profile, 0.5 * square] + gvectors + [nothing] * 3)
     vmem = pl.BlockSpec(memory_space=pltpu.VMEM)
     anywhere = pl.BlockSpec(memory_space=pl.ANY)
     steps = parts.bit_length() - 1
@@ -883,12 +999,16 @@
         out_shape=(
             jax.ShapeDtypeStruct((2, bands, local_g), bf16),
             jax.ShapeDtypeStruct((2, bands, bands), bf16),
-            jax.ShapeDtypeStruct((waters, 128), f32),
+            jax.ShapeDtypeStruct(positions.shape, f32),
         ),
         in_specs=[anywhere, vmem, vmem, vmem, vmem, vmem],
         out_specs=(anywhere, vmem, vmem),
         scratch_shapes=[
+            pltpu.VMEM((bands, 2, local_g), bf16),
             pltpu.VMEM((bands, 2 * local_g), bf16),
+            pltpu.VMEM((waters, 8 * NGRID), f32),
+            pltpu.VMEM((8, local_g), f32),
+            pltpu.VMEM((3,) + positions.shape[::2], f32),
             pltpu.VMEM((WATERS, 8 * NGRID), f32),
             pltpu.VMEM((WATERS, local_g), bf16),
             pltpu.VMEM((WATERS, local_g), bf16),
@@ -897,7 +1017,8 @@
             pltpu.VMEM((side, side), bf16),
             pltpu.VMEM((side, side), bf16),
             pltpu.VMEM((planes * block, side), f32),
-            pltpu.VMEM((CHUNKS, block, 2 * local_g), bf16),
+            pltpu.VMEM((CHUNKS, block, 2, local_g), bf16),
+            pltpu.VMEM((block, 2 * local_g), bf16),
             pltpu.VMEM((2, planes * block, side), bf16),
             pltpu.VMEM((CHUNKS, block, 2 * local_g), bf16),
             pltpu.VMEM((bands, 2 * local_g), bf16),
@@ -925,28 +1046,14 @@
             collective_id=0, has_side_effects=True, vmem_limit_bytes=67043328
         ),
     )(
-        psi[0].reshape(bands, 2 * local_g),
-        own_waves,
-        grid,
+        psi[0],
+        positions,
+        weights,
         trig_tables(),
         cross_tables(parts, planes, share),
-        vloc[0].reshape(NGRID, side),
-    )
-    turn = jnp.concatenate(
-        [
-            jnp.concatenate([mixed[0], -mixed[1]], 1),
-            jnp.concatenate([mixed[1], mixed[0]], 1),
-        ],
-        0,
-    )
-    updated = product(turn, trial.reshape(2 * bands, local_g)).astype(jnp.bfloat16)
-    psi_new = updated.reshape(2, bands, local_g).transpose(1, 0, 2)[None]
-    strength = 2.0 * occupation * nonlocal_strength / GVECS
-    oxygen_force = strength * force[:, 2:5].T
-    hydrogen_zero = jnp.zeros_like(oxygen_force)
-    dft_force = jnp.stack([oxygen_force, hydrogen_zero, hydrogen_zero], axis=2).reshape(1, 3, -1)
-    contracted_force = mixing[0][:, None, None] * dft_force
-    return (psi_new, near_forces + BEADS / CBEADS * contracted_force)
+        vloc,
+    )
+    return (rotate(mixed, trial)[None], force)
 
 
 def step_device(positions, weights, psi, vloc):

time: 301 us -> 275 us (0.914)
  local copies, waits for them, and re-layouts: 23.8 us -> 5.5 us
  Pallas kernels: 253 us -> 268 us
  matrix products: 14.9 us -> 0 us
  other arithmetic: 7.12 us -> 0 us
    pallas_call x0 -> x1, Pallas kernels: none -> 16.1 us  [rotate(): pl.pallas_call(functools.partial(rotate_kernel, (rows, local_g)), grid=(b...]
    dot_general x2 -> x0, matrix products: 14.9 us -> none  [the longest x1 13.4 us: product(): return jnp.dot(left_mat, right_mat, preferred_element_type=jnp.float32)]
    reshape x3 -> x0, local copies, waits for them, and re-layouts: 7.09 us -> none  [the longest x1 6.33 us: fused_device(): psi_new = updated.reshape(2, bands, local_g).transpose(1, 0, 2)[None]]
    slice x7 -> x0, local copies, waits for them, and re-layouts: 4.24 us -> none  [the longest x1 1.07 us: field_forces(): toward_two = positions[:, :, 2::3] - oxygen]
    unnamed x7 -> x8, local copies, waits for them, and re-layouts: 8.9 us -> 5.5 us
where the time goes in v2:
time: 275 us
  Pallas kernels  268 us (97%)
  local copies, waits for them, and re-layouts  5.5 us (2%)
    pallas_call x1, Pallas kernels, fused_device(): pl.pallas_call(functools.partial(step_kernel, (parts, bands, local_g)), o...  252 us
    pallas_call x1, Pallas kernels, rotate(): pl.pallas_call(functools.partial(rotate_kernel, (rows, local_g)), grid=(b...  16.1 us

profile of v2, /device:TPU:0, one launch (start us, length us, event | category | flops | bytes accessed | tf_op | source)
XLA Modules:
  0.0 274.6 jit_solution(16474593582422732453)
XLA Ops:
  0.6 1.5 copy.8.positions
  2.1 252.4 %shard_map.77 = (bf16[2,512,2048]{2,1,0:T(8,128)(2,1)}, bf16[2,512,512]{2,1,0:T(8,128)(2,1)}, f32[32,3,48]{2,1,0:T(4,128)}) custom-call(bf16[512,2,2048]{2,1,0:T(2,128)(2,1)} %bitcast.2, f32[32,3,48]{2,1,0:T(4,128)} %copy.8.positions, s32[1,32]{1,0:T(1,128)} %weights.1, f32[4,32,1024]{2,1,0:T(8,128)} %constant.4.clone.trig, ...), custom_call_target="tpu_custom_call" | custom-call | tf_op jit(solution)/shard_map/pallas_call | solution.py:997
  254.5 0.0 copy-start
  254.5 2.2 copy-done
  256.7 0.0 copy-start.1
  256.7 1.2 copy-done.1
  257.9 0.0 copy-start.2
  257.9 16.1 %shard_map.78 = bf16[512,2,2048]{2,1,0:T(2,128)(2,1)} custom-call(bf16[2,512,512]{2,1,0:T(8,128)(2,1)S(1)} %copy-done.1, bf16[2,512,2048]{2,1,0:T(8,128)(2,1)S(1)} %copy-done), custom_call_target="tpu_custom_call" | custom-call | tf_op jit(solution)/shard_map/pallas_call | solution.py:967
  274.0 0.0 copy-done.2
  274.0 0.6 copy.9
Async XLA Ops:
  254.5 2.2 copy-start
  256.7 1.2 copy-start.1
  257.9 16.1 %copy-start.2 = (f32[32,3,48]{2,1,0:T(4,128)S(1)}, f32[32,3,48]{2,1,0:T(4,128)}, u32[]{:S(2)}) copy-start(f32[32,3,48]{2,1,0:T(4,128)} %get-tuple-element.9) | copy-start | bytes 55300

commit v3 on v2

--- a/solution.py
+++ b/solution.py
@@ -374,8 +374,7 @@
     trig,
     cross,
     vloc,
-    trial_hbm,
-    mixed_out,
+    psi_out,
     force_out,
     raw,
     psi,
@@ -404,6 +403,7 @@
     margin,
     landing_two,
     gathered_two,
+    mixed,
     force_sum,
     force_land,
     grid_rows,
@@ -632,52 +632,72 @@
 
     lax.fori_loop(0, local_g // tile, project, 0)
 
-    def own_start(upto, rows):
+    straight = list(range(steps))
+    crossed = [0] + straight[2:] + [1]
+    narrow = bands // 2
+    single = [(0, straight, pl.ds(0, bands))]
+    double = [(1, straight, pl.ds(0, narrow)), (2, crossed, pl.ds(narrow, narrow))]
+
+    def own_start(order, upto, rows):
         start = 0
-        for bit in range(upto):
-            start = start + me // (1 << bit) % 2 * (rows >> (bit + 1))
+        for place, bit in enumerate(order[:upto]):
+            start = start + me // (1 << bit) % 2 * (rows >> (place + 1))
         return start
 
-    def sum_step(values, land, which, bit, between):
-        rows = values.shape[0]
-        half = rows >> (bit + 1)
+    def partner(bit):
         size = 1 << bit
         mine = me // size % 2
-        start = own_start(bit, rows)
-        away = pl.ds(pl.multiple_of(start + (1 - mine) * half, half), half)
-        keep = pl.ds(pl.multiple_of(start + mine * half, half), half)
+        return mine, me + (1 - 2 * mine) * size
+
+    def sum_step(values, land, halves, place, between):
+        rows = values.shape[0]
+        half = rows >> (place + 1)
         spot = pl.ds(rows - 2 * half, half)
-        copy = remote(
-            values.at[away], land.at[spot], pair(sum_sems, which, bit), me + (1 - 2 * mine) * size
-        )
-        copy.start()
+        pending = []
+        for which, order, columns in halves:
+            mine, peer = partner(order[place])
+            start = own_start(order, place, rows)
+            away = pl.ds(pl.multiple_of(start + (1 - mine) * half, half), half)
+            keep = pl.ds(pl.multiple_of(start + mine * half, half), half)
+            copy = remote(
+                values.at[away, columns],
+                land.at[spot, columns],
+                pair(sum_sems, which, place),
+                peer,
+            )
+            copy.start()
+            pending.append((copy, keep, columns))
         between()
-        copy.wait()
-        values[keep, :] += land[spot, :]
-
-    def share_step(values, which, bit, between):
+        for copy, keep, columns in pending:
+            copy.wait()
+            values[keep, columns] += land[spot, columns]
+
+    def share_step(values, halves, place, between):
         rows = values.shape[0]
-        size = 1 << bit
-        mine = me // size % 2
-        count = rows >> (bit + 1)
-        spot = pl.ds(pl.multiple_of(own_start(bit + 1, rows), count), count)
-        copy = remote(
-            values.at[spot],
-            values.at[spot],
-            pair(share_sems, which, bit),
-            me + (1 - 2 * mine) * size,
-        )
-        copy.start()
+        count = rows >> (place + 1)
+        pending = []
+        for which, order, columns in halves:
+            _, peer = partner(order[place])
+            spot = pl.ds(pl.multiple_of(own_start(order, place + 1, rows), count), count)
+            copy = remote(
+                values.at[spot, columns],
+                values.at[spot, columns],
+                pair(share_sems, which, place),
+                peer,
+            )
+            copy.start()
+            pending.append(copy)
         between()
-        copy.wait()
+        for copy in pending:
+            copy.wait()
 
     for bit in range(steps):
-        sum_step(partial, landing, 0, bit, lambda: issue(1))
+        sum_step(partial, landing, single, bit, lambda: issue(1))
     own_rows = partial.shape[0] // parts
-    own = pl.ds(pl.multiple_of(own_start(steps, partial.shape[0]), own_rows), own_rows)
+    own = pl.ds(pl.multiple_of(own_start(straight, steps, partial.shape[0]), own_rows), own_rows)
     gathered[own, :] = (partial[own, :] * (1.0 / GVECS)).astype(jnp.bfloat16)
     for bit in reversed(range(steps)):
-        share_step(gathered, 0, bit, lambda: issue(1))
+        share_step(gathered, single, bit, lambda: issue(1))
     issue(len(units))
 
     for first in range(0, gathered.shape[0], tile):
@@ -854,131 +874,93 @@
     corner_row = lax.broadcasted_iota(jnp.int32, (block, block), 0)
     corner_column = lax.broadcasted_iota(jnp.int32, (block, block), 1)
 
-    def overlap(first, second):
-        rows = pl.ds(first * block, block)
-        columns = pl.ds(second * block, block)
-
-        def even(spot):
-            return inner(trial[0, rows, spot], trial[0, columns, spot]) + inner(
-                trial[1, rows, spot], trial[1, columns, spot]
-            )
-
-        def odd(spot):
-            return inner(trial[1, rows, spot], trial[0, columns, spot]) - inner(
-                trial[0, rows, spot], trial[1, columns, spot]
-            )
-
+    def overlap(later, earlier):
+        wide = 2 * tile
+        rows = pl.ds(later * block, block)
+        columns = pl.ds(earlier * block, block)
         margin[rows, columns] = jnp.zeros((block, block), jnp.float32)
+        margin[columns, rows] = jnp.zeros((block, block), jnp.float32)
 
         def add(step, carry):
-            spot = pl.ds(pl.multiple_of(step * tile, tile), tile)
-            if first < second:
-                value = even(spot)
-            elif first > second:
-                value = odd(spot)
+            spot = pl.ds(pl.multiple_of(step * wide, wide), wide)
+            stacked = trial[:, rows, spot].reshape(2 * block, wide)
+            on_real = inner(stacked, trial[0, columns, spot])
+            on_imag = inner(stacked, trial[1, columns, spot])
+            even = on_real[:block] + on_imag[block:]
+            odd = on_real[block:] - on_imag[:block]
+            if later == earlier:
+                margin[rows, columns] += jnp.where(corner_row <= corner_column, even, odd)
             else:
-                value = jnp.where(corner_row <= corner_column, even(spot), odd(spot))
-            margin[rows, columns] += value
+                margin[columns, rows] += even
+                margin[rows, columns] += odd
             return carry
 
-        lax.fori_loop(0, local_g // tile, add, 0)
+        lax.fori_loop(0, local_g // wide, add, 0)
 
     for chunk in range(CHUNKS):
         finish(chunk)
-        trial_copy = pltpu.make_async_copy(
-            trial.at[:, pl.ds(chunk * block, block)],
-            trial_hbm.at[:, pl.ds(chunk * block, block)],
-            local_sem.at[1 + chunk],
-        )
-        trial_copy.start()
-        for first in range(chunk + 1):
-            overlap(first, chunk)
-            if first != chunk:
-                overlap(chunk, first)
-
-    for bit in range(steps):
-        sum_step(margin, landing_two, 1, bit, lambda: None)
-    start = own_start(steps, bands)
+        for earlier in range(chunk + 1):
+            overlap(chunk, earlier)
+
+    for place in range(steps):
+        sum_step(margin, landing_two, double, place, lambda: None)
     own_rows = bands // parts
-    own = pl.ds(pl.multiple_of(start, own_rows), own_rows)
-    row = start + lax.broadcasted_iota(jnp.int32, (own_rows, bands), 0)
-    column = lax.broadcasted_iota(jnp.int32, (own_rows, bands), 1)
-    mixed_rows = jnp.where(row == column, 1.5, 0.0) - (0.5 / GVECS) * margin[own, :]
-    gathered_two[own, :] = mixed_rows.astype(jnp.bfloat16)
-    for bit in reversed(range(steps)):
-        share_step(gathered_two, 1, bit, lambda: None)
-
-    for first in range(0, bands, tile):
-        for second in range(0, bands, tile):
-            there = gathered_two[first : first + tile, second : second + tile]
-            flipped = gathered_two[second : second + tile, first : first + tile]
-            there = there.astype(jnp.float32)
-            flipped = flipped.astype(jnp.float32).T
-            row = first + lax.broadcasted_iota(jnp.int32, (tile, tile), 0)
-            column = second + lax.broadcasted_iota(jnp.int32, (tile, tile), 1)
-            mix_re = jnp.where(row <= column, there, flipped)
-            mix_im = jnp.where(
-                row > column, there, jnp.where(row < column, -flipped, jnp.zeros_like(there))
-            )
-            mixed_out[0, first : first + tile, second : second + tile] = mix_re.astype(
-                jnp.bfloat16
-            )
-            mixed_out[1, first : first + tile, second : second + tile] = mix_im.astype(
-                jnp.bfloat16
-            )
+    for _, order, columns in double:
+        start = own_start(order, steps, bands)
+        own = pl.ds(pl.multiple_of(start, own_rows), own_rows)
+        row, column = spots((own_rows, narrow))
+        same = start + row == columns.start + column
+        mixed_rows = jnp.where(same, 1.5, 0.0) - (0.5 / GVECS) * margin[own, columns]
+        gathered_two[own, columns] = mixed_rows.astype(jnp.bfloat16)
+    for place in reversed(range(steps)):
+        share_step(gathered_two, double, place, lambda: None)
 
     for chunk in range(CHUNKS):
-        pltpu.make_async_copy(
-            trial.at[:, pl.ds(chunk * block, block)],
-            trial_hbm.at[:, pl.ds(chunk * block, block)],
-            local_sem.at[1 + chunk],
-        ).wait()
+        rows = pl.ds(chunk * block, block)
+        there = gathered_two[rows, rows].astype(jnp.float32)
+        flipped = there.T
+        mix_re = jnp.where(corner_row <= corner_column, there, flipped)
+        mix_im = jnp.where(
+            corner_row > corner_column,
+            there,
+            jnp.where(corner_row < corner_column, -flipped, jnp.zeros_like(there)),
+        )
+        mixed[chunk, :block, rows] = mix_re.astype(jnp.bfloat16)
+        mixed[chunk, block:, rows] = mix_im.astype(jnp.bfloat16)
+        for earlier in range(chunk):
+            columns = pl.ds(earlier * block, block)
+            even, odd = gathered_two[columns, rows], gathered_two[rows, columns]
+            mixed[chunk, :block, columns] = even
+            mixed[chunk, block:, columns] = odd
+            mixed[earlier, :block, rows] = even.astype(jnp.float32).T.astype(jnp.bfloat16)
+            mixed[earlier, block:, rows] = (-odd.astype(jnp.float32).T).astype(jnp.bfloat16)
+
+    def result_copy(chunk):
+        return pltpu.make_async_copy(
+            got.at[chunk], psi_out.at[pl.ds(chunk * block, block)], local_sem.at[1 + chunk]
+        )
+
+    for chunk in range(CHUNKS):
+
+        def turn_columns(step, carry):
+            spot = pl.ds(pl.multiple_of(step * tile, tile), tile)
+            on_real = product(mixed[chunk], trial[0, :, spot])
+            on_imag = product(mixed[chunk], trial[1, :, spot])
+            real = on_real[:block] - on_imag[block:]
+            imag = on_real[block:] + on_imag[:block]
+            got[chunk, :, 0, spot] = real.astype(jnp.bfloat16)
+            got[chunk, :, 1, spot] = imag.astype(jnp.bfloat16)
+            return carry
+
+        lax.fori_loop(0, local_g // tile, turn_columns, 0)
+        result_copy(chunk).start()
+
+    for chunk in range(CHUNKS):
+        result_copy(chunk).wait()
         each_peer(lambda turn: out_copy(chunk, turn).wait_send())
         each_peer(lambda turn: back_copy(chunk, turn).wait_send())
     each_peer(lambda turn: wave_copy(turn).wait_send())
     each_peer(lambda turn: force_copy(turn).wait_send())
-
-
-def rotate_kernel(sizes, mixed, trial_hbm, out, trial, sem):
-    rows, local_g = sizes
-    tile = 256
-    copy = pltpu.make_async_copy(trial_hbm, trial, sem.at[0])
-
-    @pl.when(pl.program_id(0) == 0)
-    def _():
-        copy.start()
-        copy.wait()
-
-    mix_re, mix_im = mixed[0], mixed[1]
-
-    def columns(step, carry):
-        spot = pl.ds(pl.multiple_of(step * tile, tile), tile)
-        real, imag = trial[0, :, spot], trial[1, :, spot]
-        out[:, 0, spot] = (product(mix_re, real) - product(mix_im, imag)).astype(out.dtype)
-        out[:, 1, spot] = (product(mix_im, real) + product(mix_re, imag)).astype(out.dtype)
-        return carry
-
-    lax.fori_loop(0, local_g // tile, columns, 0)
-
-
-def rotate(mixed, trial):
-    bands, local_g = trial.shape[1:]
-    rows = 128
-    return pl.pallas_call(
-        functools.partial(rotate_kernel, (rows, local_g)),
-        grid=(bands // rows,),
-        out_shape=jax.ShapeDtypeStruct((bands, 2, local_g), jnp.bfloat16),
-        in_specs=[
-            pl.BlockSpec((2, rows, bands), lambda step: (0, step, 0)),
-            pl.BlockSpec(memory_space=pl.ANY),
-        ],
-        out_specs=pl.BlockSpec((rows, 2, local_g), lambda step: (step, 0, 0)),
-        scratch_shapes=[
-            pltpu.VMEM(trial.shape, trial.dtype),
-            pltpu.SemaphoreType.DMA((1,)),
-        ],
-        compiler_params=pltpu.CompilerParams(vmem_limit_bytes=32 * 2**20),
-    )(mixed, trial)
 
 
 def fused_device(positions, weights, psi, vloc):
@@ -994,15 +976,14 @@
     steps = parts.bit_length() - 1
     f32, bf16 = jnp.float32, jnp.bfloat16
     dma = pltpu.SemaphoreType.DMA
-    trial, mixed, force = pl.pallas_call(
+    psi_new, force = pl.pallas_call(
         functools.partial(step_kernel, (parts, bands, local_g)),
         out_shape=(
-            jax.ShapeDtypeStruct((2, bands, local_g), bf16),
-            jax.ShapeDtypeStruct((2, bands, bands), bf16),
+            jax.ShapeDtypeStruct((bands, 2, local_g), bf16),
             jax.ShapeDtypeStruct(positions.shape, f32),
         ),
         in_specs=[anywhere, vmem, vmem, vmem, vmem, vmem],
-        out_specs=(anywhere, vmem, vmem),
+        out_specs=(anywhere, vmem),
         scratch_shapes=[
             pltpu.VMEM((bands, 2, local_g), bf16),
             pltpu.VMEM((bands, 2 * local_g), bf16),
@@ -1031,6 +1012,7 @@
             pltpu.VMEM((bands, bands), f32),
             pltpu.VMEM((bands, bands), f32),
             pltpu.VMEM((bands, bands), bf16),
+            pltpu.VMEM((CHUNKS, 2 * block, bands), bf16),
             pltpu.VMEM((WATERS, 128), f32),
             pltpu.VMEM((parts, waters, 128), f32),
             pltpu.VMEM((128, local_g), f32),
@@ -1039,8 +1021,8 @@
             dma((2, CHUNKS, parts)),
             dma((2, CHUNKS, parts)),
             dma((2, parts)),
-            dma((2, 2, steps)),
-            dma((2, 2, steps)),
+            dma((2, 3, steps)),
+            dma((2, 3, steps)),
         ],
         compiler_params=pltpu.CompilerParams(
             collective_id=0, has_side_effects=True, vmem_limit_bytes=67043328
@@ -1053,7 +1035,7 @@
         cross_tables(parts, planes, share),
         vloc,
     )
-    return (rotate(mixed, trial)[None], force)
+    return (psi_new[None], force)
 
 
 def step_device(positions, weights, psi, vloc):

time: 275 us -> 271 us (0.985)
  Pallas kernels: 268 us -> 260 us
  local copies, waits for them, and re-layouts: 5.5 us -> 10 us
    pallas_call x1 -> x0, Pallas kernels: 16.1 us -> none  [rotate(): pl.pallas_call(functools.partial(rotate_kernel, (rows, local_g)), grid=(b...]
    pallas_call x1, Pallas kernels: 252 us -> 260 us  [fused_device(): pl.pallas_call(functools.partial(step_kernel, (parts, bands, local_g)), o...]
    unnamed x8 -> x3, local copies, waits for them, and re-layouts: 5.5 us -> 10 us
where the time goes in v3:
time: 271 us; the launch traced here: 270 us
  Pallas kernels  260 us (96%)
  local copies, waits for them, and re-layouts  10 us (4%)
    pallas_call x1, Pallas kernels, fused_device(): pl.pallas_call(functools.partial(step_kernel, (parts, bands, local_g)), o...  260 us
    unnamed x3, local copies, waits for them, and re-layouts  10 us

profile of v3, /device:TPU:0, one launch (start us, length us, event | category | flops | bytes accessed | tf_op | source)
XLA Modules:
  0.0 270.4 jit_solution(7627011619732349272)
XLA Ops:
  0.6 1.5 copy.8.positions
  2.1 259.7 %shard_map.77 = (bf16[512,2,2048]{2,1,0:T(2,128)(2,1)}, f32[32,3,48]{2,1,0:T(4,128)}) custom-call(bf16[512,2,2048]{2,1,0:T(2,128)(2,1)} %bitcast.2, f32[32,3,48]{2,1,0:T(4,128)} %copy.8.positions, s32[1,32]{1,0:T(1,128)} %weights.1, f32[4,32,1024]{2,1,0:T(8,128)} %constant.4.clone.trig, bf16[2,512,512]{2,1,0:T(8,128)(2,1)} %constant.5.clone.cross, ...), custom_call_target="tpu_custom_call" | custom-call | tf_op jit(solution)/shard_map/pallas_call | solution.py:979
  261.8 1.5 copy.9
  263.3 7.1 %copy.11 = bf16[1,512,2,2048]{3,2,1,0:T(2,128)(2,1)} copy(bf16[1,512,2,2048]{3,2,1,0:T(2,128)(2,1)} %bitcast.3) | data formatting | bytes 8388608

commit v4 on v3

--- a/solution.py
+++ b/solution.py
@@ -374,11 +374,13 @@
     trig,
     cross,
     vloc,
-    psi_out,
+    trial_hbm,
+    mixed,
     force_out,
     raw,
     psi,
-    own_waves,
+    own_centres,
+    all_centres,
     grid,
     near,
     all_waves,
@@ -403,7 +405,6 @@
     margin,
     landing_two,
     gathered_two,
-    mixed,
     force_sum,
     force_land,
     grid_rows,
@@ -422,6 +423,8 @@
     block = parts * share
     steps = parts.bit_length() - 1
     tile = 256
+    atoms = positions.shape[2]
+    waters = atoms // 3
     me = lax.axis_index("ga")
 
     def other(turn):
@@ -452,9 +455,9 @@
         return sems.at[(0,) + spot], sems.at[(1,) + spot]
 
     def wave_copy(turn):
-        waters = own_waves.shape[0]
-        spot = pl.ds(pl.multiple_of(me * waters, waters), waters)
-        return remote(own_waves, all_waves.at[spot], pair(wave_sems, turn), other(turn))
+        rows = own_centres.shape[0]
+        spot = pl.ds(pl.multiple_of(me * rows, rows), rows)
+        return remote(own_centres, all_centres.at[spot], pair(wave_sems, turn), other(turn))
 
     def out_copy(chunk, turn):
         peer = other(turn)
@@ -474,7 +477,6 @@
 
     def force_copy(turn):
         peer = other(turn)
-        waters = own_waves.shape[0]
         source = pl.ds(pl.multiple_of(peer * waters, waters), waters)
         return remote(
             force_sum.at[source], force_land.at[me], pair(force_sems, turn), peer
@@ -490,8 +492,6 @@
         )
 
     each_peer(greet)
-    waters = own_waves.shape[0]
-    atoms = positions.shape[2]
     beads = positions.shape[0]
 
     def exact(left_mat, right_mat, right_axis=0):
@@ -508,18 +508,17 @@
 
     weight_row = weights[...].astype(jnp.float32)
     mixing = weight_row / jnp.sum(weight_row, axis=1, keepdims=True)
-    wave_row, wave_lane = spots(own_waves.shape)
     own_row, own_atom = spots((waters, atoms))
-    oxygen_pick = jnp.where(own_atom == 3 * own_row, 1.0, 0.0)
-    spokes = frequency(wave_lane % NGRID, NGRID)
-    angles = jnp.zeros(own_waves.shape, jnp.float32)
+    pick_row, pick_atom = spots((own_centres.shape[1], atoms))
+    oxygen_pick = jnp.where(pick_atom == 3 * pick_row, 1.0, 0.0)
+    centre_row = lax.broadcasted_iota(jnp.int32, own_centres.shape, 0)
+    near_centres = jnp.zeros(own_centres.shape, jnp.float32)
     for axis in range(3):
         centre = exact(jnp.broadcast_to(mixing, (8, beads)), positions[:, axis, :])
-        column = exact(oxygen_pick, centre, 1)[:, 0:1]
-        angles += column * jnp.where(wave_lane // (2 * NGRID) == axis, spokes, 0.0)
-    own_waves[...] = jnp.where(wave_lane // NGRID % 2 == 0, jnp.cos(angles), jnp.sin(angles))
+        near_centres += jnp.where(centre_row == axis, exact(centre, oxygen_pick, 1), 0.0)
+    own_centres[...] = near_centres
+    all_centres[pl.ds(pl.multiple_of(me * 8, 8), 8), :] = near_centres
     own_spot = pl.ds(pl.multiple_of(me * waters, waters), waters)
-    all_waves[own_spot, :] = own_waves[...]
     pl.semaphore_wait(barrier, parts - 1)
 
     units = [(chunk, far) for chunk in range(CHUNKS) for far in range(parts // 2)]
@@ -578,6 +577,25 @@
     local_psi.wait()
     lax.fori_loop(0, bands // strip, unpack_rows, 0)
     each_peer(lambda turn: wave_copy(turn).wait_recv())
+    lined = all_centres[...].T
+    _, wave_lane = spots((waters, all_waves.shape[1]))
+    spokes = frequency(wave_lane % NGRID, NGRID)
+    for source in range(parts):
+        angles = jnp.zeros(spokes.shape, jnp.float32)
+        for axis in range(3):
+            column = lined[:waters, 8 * source + axis : 8 * source + axis + 1]
+            angles += column * jnp.where(wave_lane // (2 * NGRID) == axis, spokes, 0.0)
+        all_waves[source * waters : (source + 1) * waters, :] = angles
+
+    def wave_rows(source, carry):
+        rows = pl.ds(pl.multiple_of(source * waters, waters), waters)
+        angles = all_waves[rows, :]
+        all_waves[rows, :] = jnp.where(
+            wave_lane // NGRID % 2 == 0, jnp.cos(angles), jnp.sin(angles)
+        )
+        return carry
+
+    lax.fori_loop(0, parts, wave_rows, 0)
     lane = lax.broadcasted_iota(jnp.int32, all_waves.shape, 1)
     line = lax.broadcasted_iota(jnp.int32, (all_waves.shape[1], tile), 0)
     place = lax.broadcasted_iota(jnp.int32, (all_waves.shape[1], tile), 1)
@@ -897,8 +915,15 @@
 
         lax.fori_loop(0, local_g // wide, add, 0)
 
+    def trial_copy(chunk):
+        rows = pl.ds(chunk * block, block)
+        return pltpu.make_async_copy(
+            trial.at[:, rows], trial_hbm.at[:, rows], local_sem.at[1 + chunk]
+        )
+
     for chunk in range(CHUNKS):
         finish(chunk)
+        trial_copy(chunk).start()
         for earlier in range(chunk + 1):
             overlap(chunk, earlier)
 
@@ -935,32 +960,73 @@
             mixed[earlier, :block, rows] = even.astype(jnp.float32).T.astype(jnp.bfloat16)
             mixed[earlier, block:, rows] = (-odd.astype(jnp.float32).T).astype(jnp.bfloat16)
 
-    def result_copy(chunk):
-        return pltpu.make_async_copy(
-            got.at[chunk], psi_out.at[pl.ds(chunk * block, block)], local_sem.at[1 + chunk]
-        )
-
     for chunk in range(CHUNKS):
-
-        def turn_columns(step, carry):
-            spot = pl.ds(pl.multiple_of(step * tile, tile), tile)
-            on_real = product(mixed[chunk], trial[0, :, spot])
-            on_imag = product(mixed[chunk], trial[1, :, spot])
-            real = on_real[:block] - on_imag[block:]
-            imag = on_real[block:] + on_imag[:block]
-            got[chunk, :, 0, spot] = real.astype(jnp.bfloat16)
-            got[chunk, :, 1, spot] = imag.astype(jnp.bfloat16)
-            return carry
-
-        lax.fori_loop(0, local_g // tile, turn_columns, 0)
-        result_copy(chunk).start()
-
-    for chunk in range(CHUNKS):
-        result_copy(chunk).wait()
+        trial_copy(chunk).wait()
         each_peer(lambda turn: out_copy(chunk, turn).wait_send())
         each_peer(lambda turn: back_copy(chunk, turn).wait_send())
     each_peer(lambda turn: wave_copy(turn).wait_send())
     each_peer(lambda turn: force_copy(turn).wait_send())
+
+
+def rotate_kernel(mixed_hbm, trial_hbm, out_hbm, mixed, trial, out, sems):
+    block = mixed.shape[1] // 2
+    tiles, tile = trial.shape[0], trial.shape[3]
+    mixed_copy = pltpu.make_async_copy(mixed_hbm, mixed, sems.at[tiles])
+
+    def trial_copy(step):
+        spot = pl.ds(pl.multiple_of(step * tile, tile), tile)
+        return pltpu.make_async_copy(trial_hbm.at[:, :, spot], trial.at[step], sems.at[step])
+
+    def out_copy(chunk):
+        rows = pl.ds(chunk * block, block)
+        return pltpu.make_async_copy(
+            out.at[rows], out_hbm.at[rows], sems.at[tiles + 1 + chunk]
+        )
+
+    trial_copy(0).start()
+    mixed_copy.start()
+    for step in range(1, tiles):
+        trial_copy(step).start()
+    mixed_copy.wait()
+    for chunk in range(CHUNKS):
+        rows = pl.ds(chunk * block, block)
+
+        def turn_columns(step, carry):
+            if chunk == 0:
+                trial_copy(step).wait()
+            spot = pl.ds(pl.multiple_of(step * tile, tile), tile)
+            on_real = product(mixed[chunk], trial[step, 0])
+            on_imag = product(mixed[chunk], trial[step, 1])
+            real = on_real[:block] - on_imag[block:]
+            imag = on_real[block:] + on_imag[:block]
+            out[rows, 0, spot] = real.astype(jnp.bfloat16)
+            out[rows, 1, spot] = imag.astype(jnp.bfloat16)
+            return carry
+
+        lax.fori_loop(0, tiles, turn_columns, 0)
+        out_copy(chunk).start()
+    for chunk in range(CHUNKS):
+        out_copy(chunk).wait()
+
+
+def rotate(mixed, trial):
+    bands, local_g = trial.shape[1:]
+    tile = 256
+    tiles = local_g // tile
+    anywhere = pl.BlockSpec(memory_space=pl.ANY)
+    return pl.pallas_call(
+        rotate_kernel,
+        out_shape=jax.ShapeDtypeStruct((bands, 2, local_g), jnp.bfloat16),
+        in_specs=[anywhere, anywhere],
+        out_specs=anywhere,
+        scratch_shapes=[
+            pltpu.VMEM(mixed.shape, mixed.dtype),
+            pltpu.VMEM((tiles, 2, bands, tile), trial.dtype),
+            pltpu.VMEM((bands, 2, local_g), trial.dtype),
+            pltpu.SemaphoreType.DMA((tiles + 1 + CHUNKS,)),
+        ],
+        compiler_params=pltpu.CompilerParams(vmem_limit_bytes=67043328),
+    )(mixed, trial)
 
 
 def fused_device(positions, weights, psi, vloc):
@@ -976,18 +1042,20 @@
     steps = parts.bit_length() - 1
     f32, bf16 = jnp.float32, jnp.bfloat16
     dma = pltpu.SemaphoreType.DMA
-    psi_new, force = pl.pallas_call(
+    trial, mixed, force = pl.pallas_call(
         functools.partial(step_kernel, (parts, bands, local_g)),
         out_shape=(
-            jax.ShapeDtypeStruct((bands, 2, local_g), bf16),
+            jax.ShapeDtypeStruct((2, bands, local_g), bf16),
+            jax.ShapeDtypeStruct((CHUNKS, 2 * block, bands), bf16),
             jax.ShapeDtypeStruct(positions.shape, f32),
         ),
         in_specs=[anywhere, vmem, vmem, vmem, vmem, vmem],
-        out_specs=(anywhere, vmem),
+        out_specs=(anywhere, vmem, vmem),
         scratch_shapes=[
             pltpu.VMEM((bands, 2, local_g), bf16),
             pltpu.VMEM((bands, 2 * local_g), bf16),
-            pltpu.VMEM((waters, 8 * NGRID), f32),
+            pltpu.VMEM((8, 128), f32),
+            pltpu.VMEM((parts * 8, 128), f32),
             pltpu.VMEM((8, local_g), f32),
             pltpu.VMEM((3,) + positions.shape[::2], f32),
             pltpu.VMEM((WATERS, 8 * NGRID), f32),
@@ -1012,7 +1080,6 @@
             pltpu.VMEM((bands, bands), f32),
             pltpu.VMEM((bands, bands), f32),
             pltpu.VMEM((bands, bands), bf16),
-            pltpu.VMEM((CHUNKS, 2 * block, bands), bf16),
             pltpu.VMEM((WATERS, 128), f32),
             pltpu.VMEM((parts, waters, 128), f32),
             pltpu.VMEM((128, local_g), f32),
@@ -1035,7 +1102,7 @@
         cross_tables(parts, planes, share),
         vloc,
     )
-    return (psi_new[None], force)
+    return (rotate(mixed, trial)[None], force)
 
 
 def step_device(positions, weights, psi, vloc):

time: 271 us -> 265 us (0.978)
  local copies, waits for them, and re-layouts: 10 us -> 2.93 us
    pallas_call x0 -> x1, Pallas kernels: none -> 14.2 us  [rotate(): pl.pallas_call(rotate_kernel, out_shape=jax.ShapeDtypeStruct((bands, 2, l...]
    pallas_call x1, Pallas kernels: 260 us -> 247 us  [fused_device(): pl.pallas_call(functools.partial(step_kernel, (parts, bands, local_g)), o...]
    unnamed x3 -> x2, local copies, waits for them, and re-layouts: 10 us -> 2.93 us
where the time goes in v4:
time: 265 us
  Pallas kernels  261 us (98%)
  local copies, waits for them, and re-layouts  2.93 us (1%)
    pallas_call x1, Pallas kernels, fused_device(): pl.pallas_call(functools.partial(step_kernel, (parts, bands, local_g)), o...  247 us
    pallas_call x1, Pallas kernels, rotate(): pl.pallas_call(rotate_kernel, out_shape=jax.ShapeDtypeStruct((bands, 2, l...  14.2 us

profile of v4, /device:TPU:0, one launch (start us, length us, event | category | flops | bytes accessed | tf_op | source)
XLA Modules:
  0.0 264.9 jit_solution(3728347589458076586)
XLA Ops:
  0.6 1.5 copy.8.positions
  2.1 247.1 %shard_map.77 = (bf16[2,512,2048]{2,1,0:T(8,128)(2,1)}, bf16[2,512,512]{2,1,0:T(8,128)(2,1)}, f32[32,3,48]{2,1,0:T(4,128)}) custom-call(bf16[512,2,2048]{2,1,0:T(2,128)(2,1)} %bitcast.2, f32[32,3,48]{2,1,0:T(4,128)} %copy.8.positions, s32[1,32]{1,0:T(1,128)} %weights.1, f32[4,32,1024]{2,1,0:T(8,128)} %constant.4.clone.trig, ...), custom_call_target="tpu_custom_call" | custom-call | tf_op jit(solution)/shard_map/pallas_call | solution.py:1045
  249.2 14.2 %shard_map.78 = bf16[512,2,2048]{2,1,0:T(2,128)(2,1)} custom-call(bf16[2,512,512]{2,1,0:T(8,128)(2,1)} %get-tuple-element.5.mixed_hbm, bf16[2,512,2048]{2,1,0:T(8,128)(2,1)} %get-tuple-element.6.trial_hbm), custom_call_target="tpu_custom_call" | custom-call | tf_op jit(solution)/shard_map/pallas_call | solution.py:1017
  263.4 1.5 copy.9

commit v5 on v4

--- a/solution.py
+++ b/solution.py
@@ -533,7 +533,7 @@
                     out_copy(chunk, far).start()
 
     each_peer(lambda turn: wave_copy(turn).start())
-    issue(2)
+    issue(5)
 
     flat_index = me * local_g + lax.broadcasted_iota(jnp.int32, (1, local_g), 1)
     gvectors = [

time: 265 us -> 268 us (1.011)
  Pallas kernels: 261 us -> 264 us
    pallas_call x1, Pallas kernels: 247 us -> 250 us  [fused_device(): pl.pallas_call(functools.partial(step_kernel, (parts, bands, local_g)), o...]
where the time goes in v5:
time: 268 us
  Pallas kernels  264 us (99%)
  local copies, waits for them, and re-layouts  2.93 us (1%)
    pallas_call x1, Pallas kernels, fused_device(): pl.pallas_call(functools.partial(step_kernel, (parts, bands, local_g)), o...  250 us
    pallas_call x1, Pallas kernels, rotate(): pl.pallas_call(rotate_kernel, out_shape=jax.ShapeDtypeStruct((bands, 2, l...  14.2 us

profile of v5, /device:TPU:0, one launch (start us, length us, event | category | flops | bytes accessed | tf_op | source)
XLA Modules:
  0.0 267.9 jit_solution(14467094221685274498)
XLA Ops:
  0.6 1.5 copy.8.positions
  2.1 250.1 %shard_map.77 = (bf16[2,512,2048]{2,1,0:T(8,128)(2,1)}, bf16[2,512,512]{2,1,0:T(8,128)(2,1)}, f32[32,3,48]{2,1,0:T(4,128)}) custom-call(bf16[512,2,2048]{2,1,0:T(2,128)(2,1)} %bitcast.2, f32[32,3,48]{2,1,0:T(4,128)} %copy.8.positions, s32[1,32]{1,0:T(1,128)} %weights.1, f32[4,32,1024]{2,1,0:T(8,128)} %constant.4.clone.trig, ...), custom_call_target="tpu_custom_call" | custom-call | tf_op jit(solution)/shard_map/pallas_call | solution.py:1045
  252.2 14.2 %shard_map.78 = bf16[512,2,2048]{2,1,0:T(2,128)(2,1)} custom-call(bf16[2,512,512]{2,1,0:T(8,128)(2,1)} %get-tuple-element.5.mixed_hbm, bf16[2,512,2048]{2,1,0:T(8,128)(2,1)} %get-tuple-element.6.trial_hbm), custom_call_target="tpu_custom_call" | custom-call | tf_op jit(solution)/shard_map/pallas_call | solution.py:1017
  266.4 1.5 copy.9
